TPU v7x, 128 devices: a whole 4x4x4 slice. The times are simulated.
128 devices in a mesh: seq: 8 (over y_hi, z), fsdp: 16 (over x, y_lo, core).
Axes of the slice: x: 4, y: 4 (y_hi: 2, y_lo: 2; y = y_hi * 2 + y_lo), z: 4, core: 2. Of those that a mesh axis runs over, the one named last changes fastest.
Arguments:
- queries: bfloat16 [32, 512, 8192], P('fsdp', None, 'seq'), may hold values from -48 to 48
- d_out: bfloat16 [32, 512, 8192], P('fsdp', None, 'seq'), may hold values from -12 to 12
- keys_values: bfloat16 [32, 512, 2048], P('fsdp', None, 'seq'), may hold values from -4.5 to 4.5
- lengths: int32 [32], P('fsdp'), may hold values from 1 to 512, 5461 in all
- w_kv: bfloat16 [8192, 2048], P('fsdp'), may hold values from -0.125 to 0.125
Outputs:
- d_queries: bfloat16 [32, 512, 8192], P('fsdp', 'seq')
- d_hidden: bfloat16 [32, 512, 8192], P('fsdp', 'seq')
All inputs are finite; a program needn't handle non-finite values. No bound on the sum of `lengths` on one device may be relied on, other than what follows from the above.
Results may differ from a plain program's by a relative error of at most 0.009.
Values may be sent and summed in bfloat16 or wider, within the bound.
No kernel may reach another device: no remote copies, remote signals or barrier semaphores. Data moves between devices by JAX's collectives and lax.ppermute only.
A program may use at most 128 MiB of HBM per device.

v0:
```python
import math

import jax
import jax.numpy as jnp
from jax import lax
from jax.experimental import pallas as pl
from jax.experimental.pallas import tpu as pltpu
from jax.sharding import PartitionSpec as P


HD = 128
GROUP = 8
N_SEQ = 8
BAND = 64
ROWS = N_SEQ * BAND
BI = 256
HEADS_A_STEP = 2
SCALE = 1.0 / math.sqrt(HD)
EXP2_SCALE = SCALE * math.log2(math.e)


def dot(a, b, ca, cb):
    return lax.dot_general(a, b, (((ca,), (cb,)), ((), ())), preferred_element_type=jnp.float32)


def attention_kernel(len_ref, odd_ref, q_ref, do_ref, a_ref, b_ref, dq_ref, gkv_ref, k_s, v_s, kt_s, dk_s, dv_s):
    step = pl.program_id(1)
    live = len_ref[pl.program_id(0)]

    @pl.when(step == 0)
    def _():
        @pl.when(odd_ref[0] == 0)
        def _():
            k_s[...] = a_ref[0]
            v_s[...] = b_ref[0]

        @pl.when(odd_ref[0] != 0)
        def _():
            k_s[...] = b_ref[0]
            v_s[...] = a_ref[0]

        kt_s[...] = k_s[...].T
        dk_s[...] = jnp.zeros_like(dk_s)
        dv_s[...] = jnp.zeros_like(dv_s)

    for block in range(ROWS // BI):
        lo, hi = block * BI, (block + 1) * BI
        bands = slice(lo // BAND, hi // BAND)

        @pl.when(live > lo)
        def _():
            below = lax.broadcasted_iota(jnp.int32, (BI, BI), 0) <= lax.broadcasted_iota(jnp.int32, (BI, BI), 1)
            alive = lo + lax.broadcasted_iota(jnp.int32, (1, BI), 1) < live
            for head in range(HEADS_A_STEP):
                cols = slice(head * HD, (head + 1) * HD)
                q = q_ref[0, lo:hi, cols]
                do = do_ref[0, lo:hi, cols]
                spans = ([slice(0, lo)] if lo else []) + [slice(lo, hi)]
                scores = [dot(k_s[span, :], q, 1, 1) for span in spans]
                grad_prob = [dot(v_s[span, :], do, 1, 1) for span in spans]
                scores[-1] = jnp.where(below, scores[-1], -1e30)
                largest = scores[-1].max(0, keepdims=True)
                if lo:
                    largest = jnp.maximum(largest, scores[0].max(0, keepdims=True))
                numer = [jnp.exp2((s - largest) * EXP2_SCALE) for s in scores]
                total = sum(n.sum(0, keepdims=True) for n in numer)
                inverse = jnp.where(alive, 1.0 / jnp.maximum(total, 1.0), 0.0)
                row_dot = sum((n * g).sum(0, keepdims=True) for n, g in zip(numer, grad_prob)) * inverse
                dqt = None
                for span, n, g in zip(spans, numer, grad_prob):
                    prob = n * inverse
                    grad_score = (prob * (g - row_dot)).astype(jnp.bfloat16)
                    dv_s[span, :] += dot(prob.astype(jnp.bfloat16), do, 1, 0)
                    dk_s[span, :] += dot(grad_score, q, 1, 0)
                    part = dot(kt_s[:, span], grad_score, 1, 0)
                    dqt = part if dqt is None else dqt + part
                dq = (dqt * SCALE).T.astype(jnp.bfloat16)
                dq_ref[bands, 0, :, cols] = dq.reshape(BI // BAND, BAND, HD)

        @pl.when(live <= lo)
        def _():
            dq_ref[bands] = jnp.zeros((BI // BAND, 1, BAND, HEADS_A_STEP * HD), jnp.bfloat16)

    @pl.when(step == pl.num_programs(1) - 1)
    def _():
        gkv_ref[:, 0, :, :HD] = (dk_s[...] * SCALE).astype(jnp.bfloat16).reshape(N_SEQ, BAND, HD)
        gkv_ref[:, 0, :, HD:] = dv_s[...].astype(jnp.bfloat16).reshape(N_SEQ, BAND, HD)


def attention(lengths, odd, queries, d_out, a, b):
    rollouts = queries.shape[0]
    wide = HEADS_A_STEP * HD
    rows = pl.BlockSpec((1, ROWS, wide), lambda r, h, *_: (r, 0, h))
    whole = pl.BlockSpec((1, ROWS, HD), lambda r, h, *_: (r, 0, 0))
    return pl.pallas_call(
        attention_kernel,
        out_shape=(
            jax.ShapeDtypeStruct((N_SEQ, rollouts, BAND, GROUP * HD), jnp.bfloat16),
            jax.ShapeDtypeStruct((N_SEQ, rollouts, BAND, 2 * HD), jnp.bfloat16),
        ),
        grid_spec=pltpu.PrefetchScalarGridSpec(
            num_scalar_prefetch=2,
            grid=(rollouts, GROUP // HEADS_A_STEP),
            in_specs=[rows, rows, whole, whole],
            out_specs=[
                pl.BlockSpec((N_SEQ, 1, BAND, wide), lambda r, h, *_: (0, r, 0, h)),
                pl.BlockSpec((N_SEQ, 1, BAND, 2 * HD), lambda r, h, *_: (0, r, 0, 0)),
            ],
            scratch_shapes=[
                pltpu.VMEM((ROWS, HD), jnp.bfloat16),
                pltpu.VMEM((ROWS, HD), jnp.bfloat16),
                pltpu.VMEM((HD, ROWS), jnp.bfloat16),
                pltpu.VMEM((ROWS, HD), jnp.float32),
                pltpu.VMEM((ROWS, HD), jnp.float32),
            ],
        ),
        name="attention",
    )(lengths, odd, queries, d_out, a, b)


def project_kernel(*refs):
    gs, outs, (g_s, w_s, sems) = refs[:4], refs[-7:-3], refs[-3:]
    weights = refs[4:-7]
    starts = [sum(w.shape[0] for w in weights[:i]) for i in range(len(weights) + 1)]
    spans = [slice(a, b) for a, b in zip(starts, starts[1:])]
    copies = [pltpu.make_async_copy(w, w_s.at[span], sems.at[i]) for i, (w, span) in enumerate(zip(weights, spans))]
    for copy in copies:
        copy.start()
    rows = gs[0].shape[0]
    for i, g in enumerate(gs):
        g_s[i * rows : (i + 1) * rows, :] = g[...]
    for copy, span in zip(copies, spans):
        copy.wait()
        out = dot(g_s[...], w_s[span], 1, 1).astype(jnp.bfloat16)
        for k, o in enumerate(outs):
            o[:, span] = out[k * rows : (k + 1) * rows]


def project(pieces, weights):
    rows, depth = pieces[0].shape
    cols = sum(w.shape[0] for w in weights)
    vmem = pl.BlockSpec(memory_space=pltpu.VMEM)
    return pl.pallas_call(
        project_kernel,
        out_shape=(jax.ShapeDtypeStruct((rows, cols), jnp.bfloat16),) * 4,
        in_specs=[vmem] * 4 + [pl.BlockSpec(memory_space=pl.ANY)] * len(weights),
        out_specs=[vmem] * 4,
        scratch_shapes=[
            pltpu.VMEM((4 * rows, depth), jnp.bfloat16),
            pltpu.VMEM((cols, depth), jnp.bfloat16),
            pltpu.SemaphoreType.DMA((len(weights),)),
        ],
        name="project",
    )(*pieces, *weights)


def assemble_kernel(at_ref, *refs):
    x, q = at_ref[0], at_ref[1]
    o_ref = refs[-1]
    for chunk, steps in enumerate(STEPS):
        for k in range(4):
            block = refs[4 * chunk + k]
            shard = block.shape[1] // 2
            for i, step in enumerate(steps):
                col = pl.multiple_of(((x + step) % 4 * 4 + (q ^ k)) * shard, shard)
                o_ref[:, pl.ds(col, shard)] = block[:, i * shard : (i + 1) * shard]


def assemble(at, blocks):
    rows, cols = blocks[0].shape
    vmem = pl.BlockSpec(memory_space=pltpu.VMEM)
    return pl.pallas_call(
        assemble_kernel,
        out_shape=jax.ShapeDtypeStruct((rows, 8 * cols), jnp.bfloat16),
        in_specs=[pl.BlockSpec(memory_space=pltpu.SMEM)] + [vmem] * 8,
        out_specs=vmem,
        name="assemble",
    )(at, *blocks)


X_UP = [(f, (f + 4) % 16) for f in range(16)]
X_DOWN = [(f, (f + 12) % 16) for f in range(16)]
CORE = [(f, f ^ 1) for f in range(16)]
NEAR = [(f, f ^ 2) for f in range(16)]
DIAGONAL = [(f, f ^ 3) for f in range(16)]
STEPS = ((0, 3), (1, 2))
FIRST = [(t, 2 * t) for t in range(4)] + [(4 + t, 2 * t + 1) for t in range(4)]
SECOND = [(t, 2 * t + 1) for t in range(4)] + [(4 + t, 2 * t) for t in range(4)]


def body(queries, d_out, keys_values, lengths, w_kv):
    seq = lax.axis_index("seq")
    fsdp = lax.axis_index("fsdp")
    rollouts = queries.shape[0]
    low, high = keys_values[:, :, :HD], keys_values[:, :, HD:]
    holds_keys = seq < 4
    a = lax.ppermute(jnp.where(holds_keys, low, high), "seq", FIRST)
    b = lax.ppermute(jnp.where(holds_keys, high, low), "seq", SECOND)
    half = w_kv.shape[0] // 2
    w0, w1 = w_kv[:half], w_kv[half:]
    up0 = lax.ppermute(w0, "fsdp", X_UP)
    down1 = lax.ppermute(w1, "fsdp", X_DOWN)
    up1 = lax.ppermute(w1, "fsdp", X_UP)
    down0 = lax.ppermute(w0, "fsdp", X_DOWN)
    across0 = lax.ppermute(up0, "fsdp", X_UP)
    across1 = lax.ppermute(down1, "fsdp", X_DOWN)
    odd = (seq % 2).astype(jnp.int32).reshape(1)
    at = jnp.stack([fsdp // 4, fsdp % 4]).astype(jnp.int32)
    dq, gkv = attention(lengths, odd, queries, d_out, a, b)
    gkv = lax.all_to_all(gkv, "seq", split_axis=0, concat_axis=0, tiled=True)
    dq = lax.all_to_all(dq, "seq", split_axis=0, concat_axis=0, tiled=True)
    rows = rollouts * BAND
    g = gkv.reshape(N_SEQ, rows, 2, HD).transpose(1, 2, 0, 3).reshape(rows, 2 * N_SEQ * HD)
    g_near = lax.ppermute(g, "fsdp", NEAR)
    g_core = lax.ppermute(g, "fsdp", CORE)
    g_far = lax.ppermute(g_near, "fsdp", CORE)
    pieces = (g, g_core, g_near, g_far)
    blocks = []
    for weights in ((w_kv, up0, up1), (down0, down1, across0, across1)):
        own, core, near, far = project(pieces, weights)
        near = lax.ppermute(near, "fsdp", NEAR)
        far = lax.ppermute(far, "fsdp", DIAGONAL)
        core = lax.ppermute(core, "fsdp", CORE)
        blocks += [own, core, near, far]
    d_hidden = assemble(at, blocks).reshape(rollouts, BAND, -1)
    d_queries = dq.transpose(1, 2, 0, 3).reshape(rollouts, BAND, -1)
    return d_queries, d_hidden


def solution(mesh):
    in_specs = (
        P("fsdp", None, "seq"),
        P("fsdp", None, "seq"),
        P("fsdp", None, "seq"),
        P("fsdp"),
        P("fsdp", None),
    )
    out_specs = (P("fsdp", "seq", None), P("fsdp", "seq", None))
    return jax.shard_map(body, mesh=mesh, in_specs=in_specs, out_specs=out_specs, check_vma=False)
```

profile of v0, /device:TPU:1, one launch (start us, length us, event | category | flops | bytes accessed | tf_op | source)
XLA Modules:
  0.0 139.8 jit_solution(2776778679963809499)
XLA Ops:
  2.4 5.4 %collective-permute-start.1 = (bf16[2,512,128]{2,1,0:T(8,128)(2,1)S(1)}, bf16[2,512,128]{2,1,0:T(8,128)(2,1)S(1)}, u32[]{:S(2)}, u32[]{:S(2)}) collective-permute-start(bf16[2,512,128]{2,1,0:T(8,128)(2,1)S(1)} %get-tuple-element.24), channel_id=1, source_target_pairs={{0,16},{16,48},{32,80},{48,112},{64,0},{80,32},{96,64},{112,96},{1... | collective-permute-start | bytes 786440 | tf_op jit(solution)/shard_map/ppermute | solution.py:198
  7.8 3.1 %fusion = (bf16[256,2048]{1,0:T(8,128)(2,1)}, bf16[256,2048]{1,0:T(8,128)(2,1)}) fusion(bf16[512,2048]{1,0:T(8,128)(2,1)} %refs_4_.1), kind=kLoop, calls=%fused_computation.4 | loop fusion | bytes 4194304 | tf_op jit(solution)/shard_map/slice | solution.py:200
  12.1 1.5 %collective-permute-start.11 = (bf16[256,2048]{1,0:T(8,128)(2,1)}, bf16[256,2048]{1,0:T(8,128)(2,1)}, u32[]{:S(2)}, u32[]{:S(2)}) collective-permute-start(bf16[256,2048]{1,0:T(8,128)(2,1)} %get-tuple-element.22), channel_id=1, source_target_pairs={{0,12},{1,13},{2,14},{3,15},{4,0},{5,1},{6,2},{7,3},{8,4},{9,5},{1... | collective-permute-start | bytes 3145736 | tf_op jit(solution)/shard_map/ppermute | solution.py:202
  13.6 6.5 %collective-permute-done.1.b_ref = bf16[2,512,128]{2,1,0:T(8,128)(2,1)S(1)} collective-permute-done((bf16[2,512,128]{2,1,0:T(8,128)(2,1)S(1)}, bf16[2,512,128]{2,1,0:T(8,128)(2,1)S(1)}, u32[]{:S(2)}, u32[]{:S(2)}) %collective-permute-start.1) | collective-permute-done | bytes 262176 | tf_op jit(solution)/shard_map/ppermute | solution.py:198
  20.8 11.4 %attention.1 = (bf16[8,2,64,1024]{3,2,1,0:T(8,128)(2,1)}, bf16[8,2,64,256]{3,2,1,0:T(8,128)(2,1)}) custom-call(s32[2]{0:T(128)} %len_ref.1, s32[1]{0:T(128)} %bitcast.odd_ref, bf16[2,512,1024]{2,1,0:T(8,128)(2,1)} %q_ref.1, bf16[2,512,1024]{2,1,0:T(8,128)(2,1)} %do_ref.1, bf16[2,512,128]{2,1,0:T(8,128)(2,1)} %copy-done.8, bf16[2,512,128]{2,1,0:T(8,128)(2,1)} %copy-done.9), custom_call_target="tpu_custom_call" | custom-call | tf_op jit(solution)/shard_map/attention/pallas_call | solution.py:95
  32.2 7.1 %all-to-all-start.1 = ((bf16[8,2,64,256]{3,2,1,0:T(8,128)(2,1)}), bf16[8,2,64,256]{3,2,1,0:T(8,128)(2,1)S(1)}, u32[]{:S(2)}, u32[]{:S(2)}) async-start(bf16[8,2,64,256]{3,2,1,0:T(8,128)(2,1)} %get-tuple-element.13), calls=%async_computation.1 | async-start | bytes 1048576 | tf_op jit(solution)/shard_map/all_to_all | solution.py:210
  40.6 7.4 %all-to-all-done.1 = bf16[8,2,64,256]{3,2,1,0:T(8,128)(2,1)S(1)} async-done(((bf16[8,2,64,256]{3,2,1,0:T(8,128)(2,1)}), bf16[8,2,64,256]{3,2,1,0:T(8,128)(2,1)S(1)}, u32[]{:S(2)}, u32[]{:S(2)}) %all-to-all-start.1) | async-done | bytes 524320 | tf_op jit(solution)/shard_map/all_to_all | solution.py:210
  48.0 3.6 %all-to-all-start = ((bf16[8,2,64,1024]{3,2,1,0:T(8,128)(2,1)}), bf16[8,2,64,1024]{3,2,1,0:T(8,128)(2,1)S(1)}, u32[]{:S(2)}, u32[]{:S(2)}) async-start(bf16[8,2,64,1024]{3,2,1,0:T(8,128)(2,1)} %get-tuple-element.12), calls=%async_computation | async-start | bytes 4194304 | tf_op jit(solution)/shard_map/all_to_all | solution.py:211
  52.5 5.7 %collective-permute-start.3 = (bf16[128,2048]{1,0:T(8,128)(2,1)S(1)}, bf16[128,2048]{1,0:T(8,128)(2,1)S(1)}, u32[]{:S(2)}, u32[]{:S(2)}) collective-permute-start(bf16[128,2048]{1,0:T(8,128)(2,1)S(1)} %bitcast.16), channel_id=1, source_target_pairs={{0,2},{1,3},{2,0},{3,1},{4,6},{5,7},{6,4},{7,5},{8,10},{9,11},{10,... | collective-permute-start | bytes 1572872 | tf_op jit(solution)/shard_map/ppermute | solution.py:214
  58.2 9.7 %collective-permute-start.10 = (bf16[256,2048]{1,0:T(8,128)(2,1)}, bf16[256,2048]{1,0:T(8,128)(2,1)}, u32[]{:S(2)}, u32[]{:S(2)}) collective-permute-start(bf16[256,2048]{1,0:T(8,128)(2,1)} %get-tuple-element.23), channel_id=1, source_target_pairs={{0,12},{1,13},{2,14},{3,15},{4,0},{5,1},{6,2},{7,3},{8,4},{9,5},{1... | collective-permute-start | bytes 3145736 | tf_op jit(solution)/shard_map/ppermute | solution.py:204
  67.9 2.7 %collective-permute-start.13 = (bf16[256,2048]{1,0:T(8,128)(2,1)}, bf16[256,2048]{1,0:T(8,128)(2,1)}, u32[]{:S(2)}, u32[]{:S(2)}) collective-permute-start(bf16[256,2048]{1,0:T(8,128)(2,1)} %collective-permute-done.11.refs_5_), channel_id=1, source_target_pairs={{0,12},{1,13},{2,14},{3,15},{4,0},{5,1},{6,2},{7,3},{8,4},{9,5},{1... | collective-permute-start | bytes 3145736 | tf_op jit(solution)/shard_map/ppermute | solution.py:206
  70.6 4.2 %collective-permute-done.6.refs_6_ = bf16[256,2048]{1,0:T(8,128)(2,1)} collective-permute-done((bf16[256,2048]{1,0:T(8,128)(2,1)}, bf16[256,2048]{1,0:T(8,128)(2,1)}, u32[]{:S(2)}, u32[]{:S(2)}) %collective-permute-start.6) | collective-permute-done | bytes 1048608 | tf_op jit(solution)/shard_map/ppermute | solution.py:203
  74.8 3.5 %collective-permute-start.2 = (bf16[128,2048]{1,0:T(8,128)(2,1)S(1)}, bf16[128,2048]{1,0:T(8,128)(2,1)S(1)}, u32[]{:S(2)}, u32[]{:S(2)}) collective-permute-start(bf16[128,2048]{1,0:T(8,128)(2,1)S(1)} %bitcast.17), channel_id=1, source_target_pairs={{0,1},{1,0},{2,3},{3,2},{4,5},{5,4},{6,7},{7,6},{8,9},{9,8},{10,11... | collective-permute-start | bytes 1572872 | tf_op jit(solution)/shard_map/ppermute | solution.py:215
  78.3 12.1 %collective-permute-done.3.refs_2_ = bf16[128,2048]{1,0:T(8,128)(2,1)S(1)} collective-permute-done((bf16[128,2048]{1,0:T(8,128)(2,1)S(1)}, bf16[128,2048]{1,0:T(8,128)(2,1)S(1)}, u32[]{:S(2)}, u32[]{:S(2)}) %collective-permute-start.3) | collective-permute-done | bytes 524320 | tf_op jit(solution)/shard_map/ppermute | solution.py:214
  92.4 7.8 %project.2 = (bf16[128,1024]{1,0:T(8,128)(2,1)}, bf16[128,1024]{1,0:T(8,128)(2,1)}, bf16[128,1024]{1,0:T(8,128)(2,1)}, bf16[128,1024]{1,0:T(8,128)(2,1)}) custom-call(bf16[128,2048]{1,0:T(8,128)(2,1)} %bitcast.18, bf16[128,2048]{1,0:T(8,128)(2,1)} %copy-done.2, bf16[128,2048]{1,0:T(8,128)(2,1)} %copy-done.1, ...), custom_call_target="tpu_custom_call" | custom-call | tf_op jit(solution)/shard_map/project/pallas_call | solution.py:143
  100.5 2.0 %collective-permute-start.8 = (bf16[128,1024]{1,0:T(8,128)(2,1)}, bf16[128,1024]{1,0:T(8,128)(2,1)S(1)}, u32[]{:S(2)}, u32[]{:S(2)}) collective-permute-start(bf16[128,1024]{1,0:T(8,128)(2,1)} %get-tuple-element.16), channel_id=1, source_target_pairs={{0,2},{1,3},{2,0},{3,1},{4,6},{5,7},{6,4},{7,5},{8,10},{9,11},{10,... | collective-permute-start | bytes 786440 | tf_op jit(solution)/shard_map/ppermute | solution.py:221
  102.7 5.4 %collective-permute-done.13.refs_7_ = bf16[256,2048]{1,0:T(8,128)(2,1)} collective-permute-done((bf16[256,2048]{1,0:T(8,128)(2,1)}, bf16[256,2048]{1,0:T(8,128)(2,1)}, u32[]{:S(2)}, u32[]{:S(2)}) %collective-permute-start.13) | collective-permute-done | bytes 1048608 | tf_op jit(solution)/shard_map/ppermute | solution.py:206
  108.1 8.7 %project.3 = (bf16[128,1024]{1,0:T(8,128)(2,1)}, bf16[128,1024]{1,0:T(8,128)(2,1)}, bf16[128,1024]{1,0:T(8,128)(2,1)}, bf16[128,1024]{1,0:T(8,128)(2,1)}) custom-call(bf16[128,2048]{1,0:T(8,128)(2,1)} %bitcast.19, bf16[128,2048]{1,0:T(8,128)(2,1)} %copy-done.2, bf16[128,2048]{1,0:T(8,128)(2,1)} %copy-done.1, ...), custom_call_target="tpu_custom_call" | custom-call | tf_op jit(solution)/shard_map/project/pallas_call | solution.py:143
  116.8 6.0 %collective-permute-start.14 = (bf16[128,1024]{1,0:T(8,128)(2,1)}, bf16[128,1024]{1,0:T(8,128)(2,1)S(1)}, u32[]{:S(2)}, u32[]{:S(2)}) collective-permute-start(bf16[128,1024]{1,0:T(8,128)(2,1)} %get-tuple-element.19), channel_id=1, source_target_pairs={{0,1},{1,0},{2,3},{3,2},{4,5},{5,4},{6,7},{7,6},{8,9},{9,8},{10,11... | collective-permute-start | bytes 786440 | tf_op jit(solution)/shard_map/ppermute | solution.py:223
  122.8 1.4 collective-permute-start.15
  125.2 1.6 %copy.10 = bf16[8,2,8,8,1024]{4,3,0,2,1:T(8,128)(2,1)} copy(bf16[8,2,8,8,1024]{4,3,2,1,0:T(8,128)(2,1)S(1)} %bitcast.15) | data formatting | bytes 4194304 | tf_op jit(solution)/shard_map/reshape | solution.py:226
  126.8 4.0 %collective-permute-done.15.refs_6_ = bf16[128,1024]{1,0:T(8,128)(2,1)S(1)} collective-permute-done((bf16[128,1024]{1,0:T(8,128)(2,1)}, bf16[128,1024]{1,0:T(8,128)(2,1)S(1)}, u32[]{:S(2)}, u32[]{:S(2)}) %collective-permute-start.15) | collective-permute-done | bytes 262176 | tf_op jit(solution)/shard_map/ppermute | solution.py:221
  130.8 6.0 %collective-permute-done.16.refs_7_ = bf16[128,1024]{1,0:T(8,128)(2,1)} collective-permute-done((bf16[128,1024]{1,0:T(8,128)(2,1)}, bf16[128,1024]{1,0:T(8,128)(2,1)}, u32[]{:S(2)}, u32[]{:S(2)}) %collective-permute-start.16) | collective-permute-done | bytes 262176 | tf_op jit(solution)/shard_map/ppermute | solution.py:222
  136.8 3.0 %assemble.1 = bf16[128,8192]{1,0:T(8,128)(2,1)} custom-call(s32[2]{0:T(128)} %pad_add_fusion.at_ref, bf16[128,1024]{1,0:T(8,128)(2,1)} %get-tuple-element.14.refs_0_, bf16[128,1024]{1,0:T(8,128)(2,1)} %copy-done.3, bf16[128,1024]{1,0:T(8,128)(2,1)} %copy-done.4, bf16[128,1024]{1,0:T(8,128)(2,1)} %copy-done.5, bf16[128,1024]{1,0:T(8,128)(2,1)} %get-tuple-element.18.refs_4_, ...), custom_call_target="tpu_custom_call" | custom-call | tf_op jit(solution)/shard_map/assemble/pallas_call | solution.py:172
  (45 shorter events, 9.3 us)
Async XLA Ops:
  1.7 11.9 %collective-permute-start = (bf16[2,512,128]{2,1,0:T(8,128)(2,1)S(1)}, bf16[2,512,128]{2,1,0:T(8,128)(2,1)S(1)}, u32[]{:S(2)}, u32[]{:S(2)}) collective-permute-start(bf16[2,512,128]{2,1,0:T(8,128)(2,1)S(1)} %get-tuple-element.25), channel_id=1, source_target_pairs={{0,0},{16,32},{32,64},{48,96},{64,16},{80,48},{96,80},{112,112},{1... | collective-permute-start | bytes 786440 | tf_op jit(solution)/shard_map/ppermute | solution.py:197
  2.4 17.7 %collective-permute-start.1 = (bf16[2,512,128]{2,1,0:T(8,128)(2,1)S(1)}, bf16[2,512,128]{2,1,0:T(8,128)(2,1)S(1)}, u32[]{:S(2)}, u32[]{:S(2)}) collective-permute-start(bf16[2,512,128]{2,1,0:T(8,128)(2,1)S(1)} %get-tuple-element.24), channel_id=1, source_target_pairs={{0,16},{16,48},{32,80},{48,112},{64,0},{80,32},{96,64},{112,96},{1... | collective-permute-start | bytes 786440 | tf_op jit(solution)/shard_map/ppermute | solution.py:198
  10.9 57.0 %collective-permute-start.5 = (bf16[256,2048]{1,0:T(8,128)(2,1)}, bf16[256,2048]{1,0:T(8,128)(2,1)}, u32[]{:S(2)}, u32[]{:S(2)}) collective-permute-start(bf16[256,2048]{1,0:T(8,128)(2,1)} %get-tuple-element.23), channel_id=1, source_target_pairs={{0,4},{1,5},{2,6},{3,7},{4,8},{5,9},{6,10},{7,11},{8,12},{9,13},{1... | collective-permute-start | bytes 3145736 | tf_op jit(solution)/shard_map/ppermute | solution.py:201
  12.1 55.8 %collective-permute-start.11 = (bf16[256,2048]{1,0:T(8,128)(2,1)}, bf16[256,2048]{1,0:T(8,128)(2,1)}, u32[]{:S(2)}, u32[]{:S(2)}) collective-permute-start(bf16[256,2048]{1,0:T(8,128)(2,1)} %get-tuple-element.22), channel_id=1, source_target_pairs={{0,12},{1,13},{2,14},{3,15},{4,0},{5,1},{6,2},{7,3},{8,4},{9,5},{1... | collective-permute-start | bytes 3145736 | tf_op jit(solution)/shard_map/ppermute | solution.py:202
  13.6 6.5 %copy-start.8 = (bf16[2,512,128]{2,1,0:T(8,128)(2,1)}, bf16[2,512,128]{2,1,0:T(8,128)(2,1)S(1)}, u32[]{:S(2)}) copy-start(bf16[2,512,128]{2,1,0:T(8,128)(2,1)S(1)} %collective-permute-done.a_ref) | copy-start | bytes 786436
  32.2 15.7 %all-to-all-start.1 = ((bf16[8,2,64,256]{3,2,1,0:T(8,128)(2,1)}), bf16[8,2,64,256]{3,2,1,0:T(8,128)(2,1)S(1)}, u32[]{:S(2)}, u32[]{:S(2)}) async-start(bf16[8,2,64,256]{3,2,1,0:T(8,128)(2,1)} %get-tuple-element.13), calls=%async_computation.1 | async-start | bytes 1048576 | tf_op jit(solution)/shard_map/all_to_all | solution.py:210
  39.3 35.4 %collective-permute-start.6 = (bf16[256,2048]{1,0:T(8,128)(2,1)}, bf16[256,2048]{1,0:T(8,128)(2,1)}, u32[]{:S(2)}, u32[]{:S(2)}) collective-permute-start(bf16[256,2048]{1,0:T(8,128)(2,1)} %get-tuple-element.22), channel_id=1, source_target_pairs={{0,4},{1,5},{2,6},{3,7},{4,8},{5,9},{6,10},{7,11},{8,12},{9,13},{1... | collective-permute-start | bytes 3145736 | tf_op jit(solution)/shard_map/ppermute | solution.py:203
  48.0 77.2 %all-to-all-start = ((bf16[8,2,64,1024]{3,2,1,0:T(8,128)(2,1)}), bf16[8,2,64,1024]{3,2,1,0:T(8,128)(2,1)S(1)}, u32[]{:S(2)}, u32[]{:S(2)}) async-start(bf16[8,2,64,1024]{3,2,1,0:T(8,128)(2,1)} %get-tuple-element.12), calls=%async_computation | async-start | bytes 4194304 | tf_op jit(solution)/shard_map/all_to_all | solution.py:211
  52.5 39.9 %copy-start = (bf16[16,8,16,128]{3,1,2,0:T(8,128)(2,1)}, bf16[16,8,16,128]{3,1,2,0:T(8,128)(2,1)S(1)}, u32[]{:S(2)}) copy-start(bf16[16,8,16,128]{3,1,2,0:T(8,128)(2,1)S(1)} %copy.13) | copy-start | bytes 1572868
  52.5 37.9 %collective-permute-start.3 = (bf16[128,2048]{1,0:T(8,128)(2,1)S(1)}, bf16[128,2048]{1,0:T(8,128)(2,1)S(1)}, u32[]{:S(2)}, u32[]{:S(2)}) collective-permute-start(bf16[128,2048]{1,0:T(8,128)(2,1)S(1)} %bitcast.16), channel_id=1, source_target_pairs={{0,2},{1,3},{2,0},{3,1},{4,6},{5,7},{6,4},{7,5},{8,10},{9,11},{10,... | collective-permute-start | bytes 1572872 | tf_op jit(solution)/shard_map/ppermute | solution.py:214
  58.2 44.3 %collective-permute-start.10 = (bf16[256,2048]{1,0:T(8,128)(2,1)}, bf16[256,2048]{1,0:T(8,128)(2,1)}, u32[]{:S(2)}, u32[]{:S(2)}) collective-permute-start(bf16[256,2048]{1,0:T(8,128)(2,1)} %get-tuple-element.23), channel_id=1, source_target_pairs={{0,12},{1,13},{2,14},{3,15},{4,0},{5,1},{6,2},{7,3},{8,4},{9,5},{1... | collective-permute-start | bytes 3145736 | tf_op jit(solution)/shard_map/ppermute | solution.py:204
  67.9 34.8 %collective-permute-start.12 = (bf16[256,2048]{1,0:T(8,128)(2,1)}, bf16[256,2048]{1,0:T(8,128)(2,1)}, u32[]{:S(2)}, u32[]{:S(2)}) collective-permute-start(bf16[256,2048]{1,0:T(8,128)(2,1)} %collective-permute-done.5.refs_5_), channel_id=1, source_target_pairs={{0,4},{1,5},{2,6},{3,7},{4,8},{5,9},{6,10},{7,11},{8,12},{9,13},{1... | collective-permute-start | bytes 3145736 | tf_op jit(solution)/shard_map/ppermute | solution.py:205
  67.9 40.2 %collective-permute-start.13 = (bf16[256,2048]{1,0:T(8,128)(2,1)}, bf16[256,2048]{1,0:T(8,128)(2,1)}, u32[]{:S(2)}, u32[]{:S(2)}) collective-permute-start(bf16[256,2048]{1,0:T(8,128)(2,1)} %collective-permute-done.11.refs_5_), channel_id=1, source_target_pairs={{0,12},{1,13},{2,14},{3,15},{4,0},{5,1},{6,2},{7,3},{8,4},{9,5},{1... | collective-permute-start | bytes 3145736 | tf_op jit(solution)/shard_map/ppermute | solution.py:206
  74.8 15.6 %collective-permute-start.2 = (bf16[128,2048]{1,0:T(8,128)(2,1)S(1)}, bf16[128,2048]{1,0:T(8,128)(2,1)S(1)}, u32[]{:S(2)}, u32[]{:S(2)}) collective-permute-start(bf16[128,2048]{1,0:T(8,128)(2,1)S(1)} %bitcast.17), channel_id=1, source_target_pairs={{0,1},{1,0},{2,3},{3,2},{4,5},{5,4},{6,7},{7,6},{8,9},{9,8},{10,11... | collective-permute-start | bytes 1572872 | tf_op jit(solution)/shard_map/ppermute | solution.py:215
  90.4 2.0 %collective-permute-start.4 = (bf16[128,2048]{1,0:T(8,128)(2,1)S(1)}, bf16[128,2048]{1,0:T(8,128)(2,1)}, u32[]{:S(2)}, u32[]{:S(2)}) collective-permute-start(bf16[128,2048]{1,0:T(8,128)(2,1)S(1)} %collective-permute-done.3.refs_2_), channel_id=1, source_target_pairs={{0,1},{1,0},{2,3},{3,2},{4,5},{5,4},{6,7},{7,6},{8,9},{9,8},{10,11... | collective-permute-start | bytes 1572872 | tf_op jit(solution)/shard_map/ppermute | solution.py:216
  100.2 24.0 %collective-permute-start.7 = (bf16[128,1024]{1,0:T(8,128)(2,1)}, bf16[128,1024]{1,0:T(8,128)(2,1)S(1)}, u32[]{:S(2)}, u32[]{:S(2)}) collective-permute-start(bf16[128,1024]{1,0:T(8,128)(2,1)} %get-tuple-element.15), channel_id=1, source_target_pairs={{0,1},{1,0},{2,3},{3,2},{4,5},{5,4},{6,7},{7,6},{8,9},{9,8},{10,11... | collective-permute-start | bytes 786440 | tf_op jit(solution)/shard_map/ppermute | solution.py:223
  100.5 26.2 %collective-permute-start.8 = (bf16[128,1024]{1,0:T(8,128)(2,1)}, bf16[128,1024]{1,0:T(8,128)(2,1)S(1)}, u32[]{:S(2)}, u32[]{:S(2)}) collective-permute-start(bf16[128,1024]{1,0:T(8,128)(2,1)} %get-tuple-element.16), channel_id=1, source_target_pairs={{0,2},{1,3},{2,0},{3,1},{4,6},{5,7},{6,4},{7,5},{8,10},{9,11},{10,... | collective-permute-start | bytes 786440 | tf_op jit(solution)/shard_map/ppermute | solution.py:221
  102.5 24.3 %collective-permute-start.9 = (bf16[128,1024]{1,0:T(8,128)(2,1)}, bf16[128,1024]{1,0:T(8,128)(2,1)S(1)}, u32[]{:S(2)}, u32[]{:S(2)}) collective-permute-start(bf16[128,1024]{1,0:T(8,128)(2,1)} %get-tuple-element.17), channel_id=1, source_target_pairs={{0,3},{1,2},{2,1},{3,0},{4,7},{5,6},{6,5},{7,4},{8,11},{9,10},{10,... | collective-permute-start | bytes 786440 | tf_op jit(solution)/shard_map/ppermute | solution.py:222
  116.8 9.9 %collective-permute-start.14 = (bf16[128,1024]{1,0:T(8,128)(2,1)}, bf16[128,1024]{1,0:T(8,128)(2,1)S(1)}, u32[]{:S(2)}, u32[]{:S(2)}) collective-permute-start(bf16[128,1024]{1,0:T(8,128)(2,1)} %get-tuple-element.19), channel_id=1, source_target_pairs={{0,1},{1,0},{2,3},{3,2},{4,5},{5,4},{6,7},{7,6},{8,9},{9,8},{10,11... | collective-permute-start | bytes 786440 | tf_op jit(solution)/shard_map/ppermute | solution.py:223
  122.8 8.0 %collective-permute-start.15 = (bf16[128,1024]{1,0:T(8,128)(2,1)}, bf16[128,1024]{1,0:T(8,128)(2,1)S(1)}, u32[]{:S(2)}, u32[]{:S(2)}) collective-permute-start(bf16[128,1024]{1,0:T(8,128)(2,1)} %get-tuple-element.20), channel_id=1, source_target_pairs={{0,2},{1,3},{2,0},{3,1},{4,6},{5,7},{6,4},{7,5},{8,10},{9,11},{10,... | collective-permute-start | bytes 786440 | tf_op jit(solution)/shard_map/ppermute | solution.py:221
  124.2 12.6 %collective-permute-start.16 = (bf16[128,1024]{1,0:T(8,128)(2,1)}, bf16[128,1024]{1,0:T(8,128)(2,1)}, u32[]{:S(2)}, u32[]{:S(2)}) collective-permute-start(bf16[128,1024]{1,0:T(8,128)(2,1)} %get-tuple-element.21), channel_id=1, source_target_pairs={{0,3},{1,2},{2,1},{3,0},{4,7},{5,6},{6,5},{7,4},{8,11},{9,10},{10,... | collective-permute-start | bytes 786440 | tf_op jit(solution)/shard_map/ppermute | solution.py:222
  126.7 10.1 %copy-start.4 = (bf16[128,1024]{1,0:T(8,128)(2,1)}, bf16[128,1024]{1,0:T(8,128)(2,1)S(1)}, u32[]{:S(2)}) copy-start(bf16[128,1024]{1,0:T(8,128)(2,1)S(1)} %collective-permute-done.8.refs_2_) | copy-start | bytes 786436
  126.7 10.1 %copy-start.5 = (bf16[128,1024]{1,0:T(8,128)(2,1)}, bf16[128,1024]{1,0:T(8,128)(2,1)S(1)}, u32[]{:S(2)}) copy-start(bf16[128,1024]{1,0:T(8,128)(2,1)S(1)} %collective-permute-done.9.refs_3_) | copy-start | bytes 786436
  126.7 10.0 %copy-start.6 = (bf16[128,1024]{1,0:T(8,128)(2,1)}, bf16[128,1024]{1,0:T(8,128)(2,1)S(1)}, u32[]{:S(2)}) copy-start(bf16[128,1024]{1,0:T(8,128)(2,1)S(1)} %collective-permute-done.14.refs_5_) | copy-start | bytes 786436
  (5 other events, 12.1 us)
where the time goes:
time: 141 us; the launch traced here: 140 us
  starting transfers between devices  52.4 us (37%)
  waiting for transfers between devices  46.9 us (33%)
  Pallas kernels  30.9 us (22%)
  local copies, waits for them, and re-layouts  7.09 us (5%)
  other arithmetic  1.68 us (1%)
    pallas_call x2, Pallas kernels, project(): pl.pallas_call(project_kernel, out_shape=(jax.ShapeDtypeStruct((rows, col...  16.5 us
    ppermute x1, waiting for transfers between devices, body(): g_near = lax.ppermute(g, 'fsdp', NEAR)  12.1 us
    pallas_call x1, Pallas kernels, attention(): pl.pallas_call(attention_kernel, out_shape=(jax.ShapeDtypeStruct((N_SEQ,...  11.4 us
    ppermute x1, starting transfers between devices, body(): down0 = lax.ppermute(w0, 'fsdp', X_DOWN)  9.69 us
    all_to_all x1, waiting for transfers between devices, body(): gkv = lax.all_to_all(gkv, 'seq', split_axis=0, concat_axis=0, tiled=True)  7.42 us
    all_to_all x1, starting transfers between devices, body(): gkv = lax.all_to_all(gkv, 'seq', split_axis=0, concat_axis=0, tiled=True)  7.11 us
    ppermute x1, waiting for transfers between devices, body(): b = lax.ppermute(jnp.where(holds_keys, high, low), 'seq', SECOND)  6.49 us
    ppermute x2, starting transfers between devices, body(): core = lax.ppermute(core, 'fsdp', CORE)  6.21 us
  transfers between devices with their start and end apart: 19, of which 8 were waited for; matrix products, arithmetic and copies ran while one was open for 4% of the time, Pallas kernels for 20%

commit v1 on v0

--- a/solution.py
+++ b/solution.py
@@ -13,8 +13,8 @@
 N_SEQ = 8
 BAND = 64
 ROWS = N_SEQ * BAND
-BI = 256
-HEADS_A_STEP = 2
+BI = 128
+HEADS_A_STEP = 8
 SCALE = 1.0 / math.sqrt(HD)
 EXP2_SCALE = SCALE * math.log2(math.e)
 
@@ -43,39 +43,43 @@
         dk_s[...] = jnp.zeros_like(dk_s)
         dv_s[...] = jnp.zeros_like(dv_s)
 
+    def heads_of(ref, lo, hi):
+        parts = [ref[0, lo:hi, head * HD : (head + 1) * HD] for head in range(HEADS_A_STEP)]
+        return jnp.concatenate(parts, axis=0)
+
     for block in range(ROWS // BI):
         lo, hi = block * BI, (block + 1) * BI
         bands = slice(lo // BAND, hi // BAND)
 
         @pl.when(live > lo)
         def _():
-            below = lax.broadcasted_iota(jnp.int32, (BI, BI), 0) <= lax.broadcasted_iota(jnp.int32, (BI, BI), 1)
-            alive = lo + lax.broadcasted_iota(jnp.int32, (1, BI), 1) < live
+            wide = HEADS_A_STEP * BI
+            row = lax.broadcasted_iota(jnp.int32, (1, wide), 1) % BI
+            below = lax.broadcasted_iota(jnp.int32, (BI, wide), 0) <= row
+            q, do = heads_of(q_ref, lo, hi), heads_of(do_ref, lo, hi)
+            spans = ([slice(0, lo)] if lo else []) + [slice(lo, hi)]
+            scores = [dot(k_s[span, :], q, 1, 1) for span in spans]
+            grad_prob = [dot(v_s[span, :], do, 1, 1) for span in spans]
+            scores[-1] = jnp.where(below, scores[-1], -1e30)
+            largest = scores[-1].max(0, keepdims=True)
+            if lo:
+                largest = jnp.maximum(largest, scores[0].max(0, keepdims=True))
+            numer = [jnp.exp2((s - largest) * EXP2_SCALE) for s in scores]
+            total = sum(n.sum(0, keepdims=True) for n in numer)
+            inverse = jnp.where(lo + row < live, 1.0 / jnp.maximum(total, 1.0), 0.0)
+            row_dot = sum((n * g).sum(0, keepdims=True) for n, g in zip(numer, grad_prob)) * inverse
+            dqt = None
+            for span, n, g in zip(spans, numer, grad_prob):
+                prob = n * inverse
+                grad_score = (prob * (g - row_dot)).astype(jnp.bfloat16)
+                dv_s[span, :] += dot(prob.astype(jnp.bfloat16), do, 1, 0)
+                dk_s[span, :] += dot(grad_score, q, 1, 0)
+                part = dot(kt_s[:, span], grad_score, 1, 0)
+                dqt = part if dqt is None else dqt + part
+            dqt = dqt * SCALE
             for head in range(HEADS_A_STEP):
-                cols = slice(head * HD, (head + 1) * HD)
-                q = q_ref[0, lo:hi, cols]
-                do = do_ref[0, lo:hi, cols]
-                spans = ([slice(0, lo)] if lo else []) + [slice(lo, hi)]
-                scores = [dot(k_s[span, :], q, 1, 1) for span in spans]
-                grad_prob = [dot(v_s[span, :], do, 1, 1) for span in spans]
-                scores[-1] = jnp.where(below, scores[-1], -1e30)
-                largest = scores[-1].max(0, keepdims=True)
-                if lo:
-                    largest = jnp.maximum(largest, scores[0].max(0, keepdims=True))
-                numer = [jnp.exp2((s - largest) * EXP2_SCALE) for s in scores]
-                total = sum(n.sum(0, keepdims=True) for n in numer)
-                inverse = jnp.where(alive, 1.0 / jnp.maximum(total, 1.0), 0.0)
-                row_dot = sum((n * g).sum(0, keepdims=True) for n, g in zip(numer, grad_prob)) * inverse
-                dqt = None
-                for span, n, g in zip(spans, numer, grad_prob):
-                    prob = n * inverse
-                    grad_score = (prob * (g - row_dot)).astype(jnp.bfloat16)
-                    dv_s[span, :] += dot(prob.astype(jnp.bfloat16), do, 1, 0)
-                    dk_s[span, :] += dot(grad_score, q, 1, 0)
-                    part = dot(kt_s[:, span], grad_score, 1, 0)
-                    dqt = part if dqt is None else dqt + part
-                dq = (dqt * SCALE).T.astype(jnp.bfloat16)
-                dq_ref[bands, 0, :, cols] = dq.reshape(BI // BAND, BAND, HD)
+                dq = dqt[:, head * BI : (head + 1) * BI].T.astype(jnp.bfloat16)
+                dq_ref[bands, 0, :, head * HD : (head + 1) * HD] = dq.reshape(BI // BAND, BAND, HD)
 
         @pl.when(live <= lo)
         def _():
@@ -121,14 +125,15 @@
 def project_kernel(*refs):
     gs, outs, (g_s, w_s, sems) = refs[:4], refs[-7:-3], refs[-3:]
     weights = refs[4:-7]
+    rows = gs[0].shape[0]
     starts = [sum(w.shape[0] for w in weights[:i]) for i in range(len(weights) + 1)]
     spans = [slice(a, b) for a, b in zip(starts, starts[1:])]
-    copies = [pltpu.make_async_copy(w, w_s.at[span], sems.at[i]) for i, (w, span) in enumerate(zip(weights, spans))]
-    for copy in copies:
+    loads = [pltpu.make_async_copy(g, g_s.at[i * rows : (i + 1) * rows], sems.at[i]) for i, g in enumerate(gs)]
+    copies = [pltpu.make_async_copy(w, w_s.at[span], sems.at[4 + i]) for i, (w, span) in enumerate(zip(weights, spans))]
+    for copy in loads + copies:
         copy.start()
-    rows = gs[0].shape[0]
-    for i, g in enumerate(gs):
-        g_s[i * rows : (i + 1) * rows, :] = g[...]
+    for copy in loads:
+        copy.wait()
     for copy, span in zip(copies, spans):
         copy.wait()
         out = dot(g_s[...], w_s[span], 1, 1).astype(jnp.bfloat16)
@@ -139,16 +144,16 @@
 def project(pieces, weights):
     rows, depth = pieces[0].shape
     cols = sum(w.shape[0] for w in weights)
-    vmem = pl.BlockSpec(memory_space=pltpu.VMEM)
+    stay = pl.BlockSpec(memory_space=pl.ANY)
     return pl.pallas_call(
         project_kernel,
         out_shape=(jax.ShapeDtypeStruct((rows, cols), jnp.bfloat16),) * 4,
-        in_specs=[vmem] * 4 + [pl.BlockSpec(memory_space=pl.ANY)] * len(weights),
-        out_specs=[vmem] * 4,
+        in_specs=[stay] * (4 + len(weights)),
+        out_specs=[pl.BlockSpec(memory_space=pltpu.VMEM)] * 4,
         scratch_shapes=[
             pltpu.VMEM((4 * rows, depth), jnp.bfloat16),
             pltpu.VMEM((cols, depth), jnp.bfloat16),
-            pltpu.SemaphoreType.DMA((len(weights),)),
+            pltpu.SemaphoreType.DMA((4 + len(weights),)),
         ],
         name="project",
     )(*pieces, *weights)
@@ -160,19 +165,20 @@
     for chunk, steps in enumerate(STEPS):
         for k in range(4):
             block = refs[4 * chunk + k]
-            shard = block.shape[1] // 2
+            shard = block.shape[1] // len(steps)
             for i, step in enumerate(steps):
                 col = pl.multiple_of(((x + step) % 4 * 4 + (q ^ k)) * shard, shard)
                 o_ref[:, pl.ds(col, shard)] = block[:, i * shard : (i + 1) * shard]
 
 
 def assemble(at, blocks):
-    rows, cols = blocks[0].shape
+    rows = blocks[0].shape[0]
+    cols = sum(block.shape[1] for block in blocks)
     vmem = pl.BlockSpec(memory_space=pltpu.VMEM)
     return pl.pallas_call(
         assemble_kernel,
-        out_shape=jax.ShapeDtypeStruct((rows, 8 * cols), jnp.bfloat16),
-        in_specs=[pl.BlockSpec(memory_space=pltpu.SMEM)] + [vmem] * 8,
+        out_shape=jax.ShapeDtypeStruct((rows, cols), jnp.bfloat16),
+        in_specs=[pl.BlockSpec(memory_space=pltpu.SMEM)] + [vmem] * len(blocks),
         out_specs=vmem,
         name="assemble",
     )(at, *blocks)
@@ -183,7 +189,7 @@
 CORE = [(f, f ^ 1) for f in range(16)]
 NEAR = [(f, f ^ 2) for f in range(16)]
 DIAGONAL = [(f, f ^ 3) for f in range(16)]
-STEPS = ((0, 3), (1, 2))
+STEPS = ((0, 3, 1), (2,))
 FIRST = [(t, 2 * t) for t in range(4)] + [(4 + t, 2 * t + 1) for t in range(4)]
 SECOND = [(t, 2 * t + 1) for t in range(4)] + [(4 + t, 2 * t) for t in range(4)]
 
@@ -216,7 +222,7 @@
     g_far = lax.ppermute(g_near, "fsdp", CORE)
     pieces = (g, g_core, g_near, g_far)
     blocks = []
-    for weights in ((w_kv, up0, up1), (down0, down1, across0, across1)):
+    for weights in ((w_kv, up0, up1, down0, down1), (across0, across1)):
         own, core, near, far = project(pieces, weights)
         near = lax.ppermute(near, "fsdp", NEAR)
         far = lax.ppermute(far, "fsdp", DIAGONAL)

time: 141 us -> 136 us (0.965)
  waiting for transfers between devices: 46.9 us -> 57.9 us
  Pallas kernels: 30.9 us -> 23.4 us
  starting transfers between devices: 52.4 us -> 46.1 us
  local copies, waits for them, and re-layouts: 7.09 us -> 5.51 us
    ppermute x1, waiting for transfers between devices: 4.23 us -> 19.8 us  [body(): up1 = lax.ppermute(w1, 'fsdp', X_UP)]
    ppermute x1, waiting for transfers between devices: 12.1 us -> 0.01 us  [body(): g_near = lax.ppermute(g, 'fsdp', NEAR)]
    ppermute x1, waiting for transfers between devices: 0.01 us -> 10.6 us  [body(): up0 = lax.ppermute(w0, 'fsdp', X_UP)]
    ppermute x1, starting transfers between devices: 1.47 us -> 10.3 us  [body(): down1 = lax.ppermute(w1, 'fsdp', X_DOWN)]
    all_to_all x1, waiting for transfers between devices: 7.42 us -> 0.01 us  [body(): gkv = lax.all_to_all(gkv, 'seq', split_axis=0, concat_axis=0, tiled=True)]
    ppermute x1, waiting for transfers between devices: 0.01 us -> 6.78 us  [body(): across0 = lax.ppermute(up0, 'fsdp', X_UP)]
    ppermute x2, starting transfers between devices: 6.21 us -> 0.31 us  [body(): core = lax.ppermute(core, 'fsdp', CORE)]
    pallas_call x1, Pallas kernels: 11.4 us -> 5.6 us  [attention(): pl.pallas_call(attention_kernel, out_shape=(jax.ShapeDtypeStruct((N_SEQ,...]
  transfers between devices with their start and end apart: 19 -> 19, of which waited for: 8 -> 9; matrix products, arithmetic and copies ran while one was open for 4% -> 3% of each run, Pallas kernels for 20% -> 11%
where the time goes in v1:
time: 136 us; the launch traced here: 135 us
  waiting for transfers between devices  57.9 us (43%)
  starting transfers between devices  46.1 us (34%)
  Pallas kernels  23.4 us (17%)
  local copies, waits for them, and re-layouts  5.51 us (4%)
  other arithmetic  1.62 us (1%)
    ppermute x1, waiting for transfers between devices, body(): up1 = lax.ppermute(w1, 'fsdp', X_UP)  19.8 us
    pallas_call x2, Pallas kernels, project(): pl.pallas_call(project_kernel, out_shape=(jax.ShapeDtypeStruct((rows, col...  14.9 us
    ppermute x1, waiting for transfers between devices, body(): b = lax.ppermute(jnp.where(holds_keys, high, low), 'seq', SECOND)  12.3 us
    ppermute x1, waiting for transfers between devices, body(): up0 = lax.ppermute(w0, 'fsdp', X_UP)  10.6 us
    ppermute x1, starting transfers between devices, body(): down1 = lax.ppermute(w1, 'fsdp', X_DOWN)  10.3 us
    all_to_all x1, starting transfers between devices, body(): gkv = lax.all_to_all(gkv, 'seq', split_axis=0, concat_axis=0, tiled=True)  7.11 us
    ppermute x1, waiting for transfers between devices, body(): across0 = lax.ppermute(up0, 'fsdp', X_UP)  6.78 us
    all_to_all x1, starting transfers between devices, body(): dq = lax.all_to_all(dq, 'seq', split_axis=0, concat_axis=0, tiled=True)  6.65 us
  transfers between devices with their start and end apart: 19, of which 9 were waited for; matrix products, arithmetic and copies ran while one was open for 3% of the time, Pallas kernels for 11%

profile of v1, /device:TPU:1, one launch (start us, length us, event | category | flops | bytes accessed | tf_op | source)
XLA Modules:
  0.0 135.3 jit_solution(7799102715556922330)
XLA Ops:
  0.6 1.1 broadcast_select_fusion
  2.4 5.4 %collective-permute-start.1 = (bf16[2,512,128]{2,1,0:T(8,128)(2,1)S(1)}, bf16[2,512,128]{2,1,0:T(8,128)(2,1)S(1)}, u32[]{:S(2)}, u32[]{:S(2)}) collective-permute-start(bf16[2,512,128]{2,1,0:T(8,128)(2,1)S(1)} %get-tuple-element.24), channel_id=1, source_target_pairs={{0,16},{16,48},{32,80},{48,112},{64,0},{80,32},{96,64},{112,96},{1... | collective-permute-start | bytes 786440 | tf_op jit(solution)/shard_map/ppermute | solution.py:204
  7.8 12.3 %collective-permute-done.1.b_ref = bf16[2,512,128]{2,1,0:T(8,128)(2,1)S(1)} collective-permute-done((bf16[2,512,128]{2,1,0:T(8,128)(2,1)S(1)}, bf16[2,512,128]{2,1,0:T(8,128)(2,1)S(1)}, u32[]{:S(2)}, u32[]{:S(2)}) %collective-permute-start.1) | collective-permute-done | bytes 262176 | tf_op jit(solution)/shard_map/ppermute | solution.py:204
  20.8 5.6 %attention.1 = (bf16[8,2,64,1024]{3,2,1,0:T(8,128)(2,1)}, bf16[8,2,64,256]{3,2,1,0:T(8,128)(2,1)}) custom-call(s32[2]{0:T(128)} %len_ref.1, s32[1]{0:T(128)} %bitcast.odd_ref, bf16[2,512,1024]{2,1,0:T(8,128)(2,1)} %q_ref.1, bf16[2,512,1024]{2,1,0:T(8,128)(2,1)} %do_ref.1, bf16[2,512,128]{2,1,0:T(8,128)(2,1)} %copy-done.7, bf16[2,512,128]{2,1,0:T(8,128)(2,1)} %copy-done.8), custom_call_target="tpu_custom_call" | custom-call | tf_op jit(solution)/shard_map/attention/pallas_call | solution.py:99
  26.4 7.1 %all-to-all-start.1 = ((bf16[8,2,64,256]{3,2,1,0:T(8,128)(2,1)}), bf16[8,2,64,256]{3,2,1,0:T(8,128)(2,1)S(1)}, u32[]{:S(2)}, u32[]{:S(2)}) async-start(bf16[8,2,64,256]{3,2,1,0:T(8,128)(2,1)} %get-tuple-element.13), calls=%async_computation.1 | async-start | bytes 1048576 | tf_op jit(solution)/shard_map/all_to_all | solution.py:216
  33.5 1.6 %fusion = (bf16[256,2048]{1,0:T(8,128)(2,1)}, bf16[256,2048]{1,0:T(8,128)(2,1)}) fusion(bf16[512,2048]{1,0:T(8,128)(2,1)S(1)} %copy-done), kind=kLoop, calls=%fused_computation.4 | loop fusion | bytes 4194304 | tf_op jit(solution)/shard_map/slice | solution.py:206
  35.1 2.5 %collective-permute-start.5 = (bf16[256,2048]{1,0:T(8,128)(2,1)}, bf16[256,2048]{1,0:T(8,128)(2,1)}, u32[]{:S(2)}, u32[]{:S(2)}) collective-permute-start(bf16[256,2048]{1,0:T(8,128)(2,1)} %get-tuple-element.23), channel_id=1, source_target_pairs={{0,4},{1,5},{2,6},{3,7},{4,8},{5,9},{6,10},{7,11},{8,12},{9,13},{1... | collective-permute-start | bytes 3145736 | tf_op jit(solution)/shard_map/ppermute | solution.py:207
  37.5 10.3 %collective-permute-start.8 = (bf16[256,2048]{1,0:T(8,128)(2,1)}, bf16[256,2048]{1,0:T(8,128)(2,1)}, u32[]{:S(2)}, u32[]{:S(2)}) collective-permute-start(bf16[256,2048]{1,0:T(8,128)(2,1)} %get-tuple-element.22), channel_id=1, source_target_pairs={{0,12},{1,13},{2,14},{3,15},{4,0},{5,1},{6,2},{7,3},{8,4},{9,5},{1... | collective-permute-start | bytes 3145736 | tf_op jit(solution)/shard_map/ppermute | solution.py:208
  47.9 6.6 %all-to-all-start = ((bf16[8,2,64,1024]{3,2,1,0:T(8,128)(2,1)}), bf16[8,2,64,1024]{3,2,1,0:T(8,128)(2,1)S(1)}, u32[]{:S(2)}, u32[]{:S(2)}) async-start(bf16[8,2,64,1024]{3,2,1,0:T(8,128)(2,1)} %get-tuple-element.12), calls=%async_computation | async-start | bytes 4194304 | tf_op jit(solution)/shard_map/all_to_all | solution.py:217
  54.5 5.8 %collective-permute-start.7 = (bf16[256,2048]{1,0:T(8,128)(2,1)}, bf16[256,2048]{1,0:T(8,128)(2,1)}, u32[]{:S(2)}, u32[]{:S(2)}) collective-permute-start(bf16[256,2048]{1,0:T(8,128)(2,1)} %get-tuple-element.23), channel_id=1, source_target_pairs={{0,12},{1,13},{2,14},{3,15},{4,0},{5,1},{6,2},{7,3},{8,4},{9,5},{1... | collective-permute-start | bytes 3145736 | tf_op jit(solution)/shard_map/ppermute | solution.py:210
  61.3 10.6 %collective-permute-done.5.refs_5_ = bf16[256,2048]{1,0:T(8,128)(2,1)} collective-permute-done((bf16[256,2048]{1,0:T(8,128)(2,1)}, bf16[256,2048]{1,0:T(8,128)(2,1)}, u32[]{:S(2)}, u32[]{:S(2)}) %collective-permute-start.5) | collective-permute-done | bytes 1048608 | tf_op jit(solution)/shard_map/ppermute | solution.py:207
  71.9 2.7 %collective-permute-start.13 = (bf16[256,2048]{1,0:T(8,128)(2,1)}, bf16[256,2048]{1,0:T(8,128)(2,1)}, u32[]{:S(2)}, u32[]{:S(2)}) collective-permute-start(bf16[256,2048]{1,0:T(8,128)(2,1)} %collective-permute-done.8.refs_8_), channel_id=1, source_target_pairs={{0,12},{1,13},{2,14},{3,15},{4,0},{5,1},{6,2},{7,3},{8,4},{9,5},{1... | collective-permute-start | bytes 3145736 | tf_op jit(solution)/shard_map/ppermute | solution.py:212
  74.6 19.8 %collective-permute-done.6.refs_6_ = bf16[256,2048]{1,0:T(8,128)(2,1)} collective-permute-done((bf16[256,2048]{1,0:T(8,128)(2,1)}, bf16[256,2048]{1,0:T(8,128)(2,1)}, u32[]{:S(2)}, u32[]{:S(2)}) %collective-permute-start.6) | collective-permute-done | bytes 1048608 | tf_op jit(solution)/shard_map/ppermute | solution.py:209
  94.9 1.4 %collective-permute-done.2.refs_1_ = bf16[128,2048]{1,0:T(8,128)(2,1)S(1)} collective-permute-done((bf16[128,2048]{1,0:T(8,128)(2,1)S(1)}, bf16[128,2048]{1,0:T(8,128)(2,1)S(1)}, u32[]{:S(2)}, u32[]{:S(2)}) %collective-permute-start.2) | collective-permute-done | bytes 524320 | tf_op jit(solution)/shard_map/ppermute | solution.py:221
  97.2 9.7 %project.2 = (bf16[128,1536]{1,0:T(8,128)(2,1)}, bf16[128,1536]{1,0:T(8,128)(2,1)}, bf16[128,1536]{1,0:T(8,128)(2,1)}, bf16[128,1536]{1,0:T(8,128)(2,1)}) custom-call(bf16[128,2048]{1,0:T(8,128)(2,1)} %bitcast.18, bf16[128,2048]{1,0:T(8,128)(2,1)} %copy-done.3, bf16[128,2048]{1,0:T(8,128)(2,1)} %copy-done.2, ...), custom_call_target="tpu_custom_call" | custom-call | tf_op jit(solution)/shard_map/project/pallas_call | solution.py:148
  107.1 2.0 %collective-permute-start.11 = (bf16[128,1536]{1,0:T(8,128)(2,1)}, bf16[128,1536]{1,0:T(8,128)(2,1)S(1)}, u32[]{:S(2)}, u32[]{:S(2)}) collective-permute-start(bf16[128,1536]{1,0:T(8,128)(2,1)} %get-tuple-element.17), channel_id=1, source_target_pairs={{0,3},{1,2},{2,1},{3,0},{4,7},{5,6},{6,5},{7,4},{8,11},{9,10},{10,... | collective-permute-start | bytes 1179656 | tf_op jit(solution)/shard_map/ppermute | solution.py:228
  109.1 6.8 %collective-permute-done.12.refs_4_ = bf16[256,2048]{1,0:T(8,128)(2,1)} collective-permute-done((bf16[256,2048]{1,0:T(8,128)(2,1)}, bf16[256,2048]{1,0:T(8,128)(2,1)}, u32[]{:S(2)}, u32[]{:S(2)}) %collective-permute-start.12) | collective-permute-done | bytes 1048608 | tf_op jit(solution)/shard_map/ppermute | solution.py:211
  115.9 5.2 %project.3 = (bf16[128,512]{1,0:T(8,128)(2,1)}, bf16[128,512]{1,0:T(8,128)(2,1)}, bf16[128,512]{1,0:T(8,128)(2,1)}, bf16[128,512]{1,0:T(8,128)(2,1)}) custom-call(bf16[128,2048]{1,0:T(8,128)(2,1)} %bitcast.19, bf16[128,2048]{1,0:T(8,128)(2,1)} %copy-done.3, bf16[128,2048]{1,0:T(8,128)(2,1)} %copy-done.2, bf16[128,2048]{1,0:T(8,128)(2,1)} %collective-permute-done.4.refs_3_, ...), custom_call_target="tpu_custom_call" | custom-call | tf_op jit(solution)/shard_map/project/pallas_call | solution.py:148
  121.3 2.0 %collective-permute-start.16 = (bf16[128,512]{1,0:T(8,128)(2,1)}, bf16[128,512]{1,0:T(8,128)(2,1)}, u32[]{:S(2)}, u32[]{:S(2)}) collective-permute-start(bf16[128,512]{1,0:T(8,128)(2,1)} %get-tuple-element.21), channel_id=1, source_target_pairs={{0,3},{1,2},{2,1},{3,0},{4,7},{5,6},{6,5},{7,4},{8,11},{9,10},{10,... | collective-permute-start | bytes 393224 | tf_op jit(solution)/shard_map/ppermute | solution.py:228
  123.8 1.6 %copy.10 = bf16[8,2,8,8,1024]{4,3,0,2,1:T(8,128)(2,1)} copy(bf16[8,2,8,8,1024]{4,3,2,1,0:T(8,128)(2,1)S(1)} %bitcast.15) | data formatting | bytes 4194304 | tf_op jit(solution)/shard_map/reshape | solution.py:232
  125.4 2.0 %collective-permute-done.11.refs_3_ = bf16[128,1536]{1,0:T(8,128)(2,1)S(1)} collective-permute-done((bf16[128,1536]{1,0:T(8,128)(2,1)}, bf16[128,1536]{1,0:T(8,128)(2,1)S(1)}, u32[]{:S(2)}, u32[]{:S(2)}) %collective-permute-start.11) | collective-permute-done | bytes 393248 | tf_op jit(solution)/shard_map/ppermute | solution.py:228
  127.4 1.4 %collective-permute-done.15.refs_6_ = bf16[128,512]{1,0:T(8,128)(2,1)S(1)} collective-permute-done((bf16[128,512]{1,0:T(8,128)(2,1)}, bf16[128,512]{1,0:T(8,128)(2,1)S(1)}, u32[]{:S(2)}, u32[]{:S(2)}) %collective-permute-start.15) | collective-permute-done | bytes 131104 | tf_op jit(solution)/shard_map/ppermute | solution.py:227
  128.8 3.5 %collective-permute-done.16.refs_7_ = bf16[128,512]{1,0:T(8,128)(2,1)} collective-permute-done((bf16[128,512]{1,0:T(8,128)(2,1)}, bf16[128,512]{1,0:T(8,128)(2,1)}, u32[]{:S(2)}, u32[]{:S(2)}) %collective-permute-start.16) | collective-permute-done | bytes 131104 | tf_op jit(solution)/shard_map/ppermute | solution.py:228
  132.3 3.0 %assemble.1 = bf16[128,8192]{1,0:T(8,128)(2,1)} custom-call(s32[2]{0:T(128)} %pad_add_fusion.at_ref, bf16[128,1536]{1,0:T(8,128)(2,1)} %get-tuple-element.14.refs_0_, bf16[128,1536]{1,0:T(8,128)(2,1)} %copy-done.4, bf16[128,1536]{1,0:T(8,128)(2,1)} %copy-done.5, bf16[128,1536]{1,0:T(8,128)(2,1)} %copy-done.6, bf16[128,512]{1,0:T(8,128)(2,1)} %get-tuple-element.18.refs_4_, ...), custom_call_target="tpu_custom_call" | custom-call | tf_op jit(solution)/shard_map/assemble/pallas_call | solution.py:178
  (47 shorter events, 4.7 us)
Async XLA Ops:
  1.7 6.1 %collective-permute-start = (bf16[2,512,128]{2,1,0:T(8,128)(2,1)S(1)}, bf16[2,512,128]{2,1,0:T(8,128)(2,1)S(1)}, u32[]{:S(2)}, u32[]{:S(2)}) collective-permute-start(bf16[2,512,128]{2,1,0:T(8,128)(2,1)S(1)} %get-tuple-element.25), channel_id=1, source_target_pairs={{0,0},{16,32},{32,64},{48,96},{64,16},{80,48},{96,80},{112,112},{1... | collective-permute-start | bytes 786440 | tf_op jit(solution)/shard_map/ppermute | solution.py:203
  2.4 17.7 %collective-permute-start.1 = (bf16[2,512,128]{2,1,0:T(8,128)(2,1)S(1)}, bf16[2,512,128]{2,1,0:T(8,128)(2,1)S(1)}, u32[]{:S(2)}, u32[]{:S(2)}) collective-permute-start(bf16[2,512,128]{2,1,0:T(8,128)(2,1)S(1)} %get-tuple-element.24), channel_id=1, source_target_pairs={{0,16},{16,48},{32,80},{48,112},{64,0},{80,32},{96,64},{112,96},{1... | collective-permute-start | bytes 786440 | tf_op jit(solution)/shard_map/ppermute | solution.py:204
  7.8 12.3 %copy-start.7 = (bf16[2,512,128]{2,1,0:T(8,128)(2,1)}, bf16[2,512,128]{2,1,0:T(8,128)(2,1)S(1)}, u32[]{:S(2)}) copy-start(bf16[2,512,128]{2,1,0:T(8,128)(2,1)S(1)} %collective-permute-done.a_ref) | copy-start | bytes 786436
  20.8 12.7 %copy-start = (bf16[512,2048]{1,0:T(8,128)(2,1)S(1)}, bf16[512,2048]{1,0:T(8,128)(2,1)}, u32[]{:S(2)}) copy-start(bf16[512,2048]{1,0:T(8,128)(2,1)} %refs_4_.1) | copy-start | bytes 6291460
  26.4 21.5 %all-to-all-start.1 = ((bf16[8,2,64,256]{3,2,1,0:T(8,128)(2,1)}), bf16[8,2,64,256]{3,2,1,0:T(8,128)(2,1)S(1)}, u32[]{:S(2)}, u32[]{:S(2)}) async-start(bf16[8,2,64,256]{3,2,1,0:T(8,128)(2,1)} %get-tuple-element.13), calls=%async_computation.1 | async-start | bytes 1048576 | tf_op jit(solution)/shard_map/all_to_all | solution.py:216
  35.1 36.8 %collective-permute-start.5 = (bf16[256,2048]{1,0:T(8,128)(2,1)}, bf16[256,2048]{1,0:T(8,128)(2,1)}, u32[]{:S(2)}, u32[]{:S(2)}) collective-permute-start(bf16[256,2048]{1,0:T(8,128)(2,1)} %get-tuple-element.23), channel_id=1, source_target_pairs={{0,4},{1,5},{2,6},{3,7},{4,8},{5,9},{6,10},{7,11},{8,12},{9,13},{1... | collective-permute-start | bytes 3145736 | tf_op jit(solution)/shard_map/ppermute | solution.py:207
  37.5 34.4 %collective-permute-start.8 = (bf16[256,2048]{1,0:T(8,128)(2,1)}, bf16[256,2048]{1,0:T(8,128)(2,1)}, u32[]{:S(2)}, u32[]{:S(2)}) collective-permute-start(bf16[256,2048]{1,0:T(8,128)(2,1)} %get-tuple-element.22), channel_id=1, source_target_pairs={{0,12},{1,13},{2,14},{3,15},{4,0},{5,1},{6,2},{7,3},{8,4},{9,5},{1... | collective-permute-start | bytes 3145736 | tf_op jit(solution)/shard_map/ppermute | solution.py:208
  47.9 46.5 %collective-permute-start.6 = (bf16[256,2048]{1,0:T(8,128)(2,1)}, bf16[256,2048]{1,0:T(8,128)(2,1)}, u32[]{:S(2)}, u32[]{:S(2)}) collective-permute-start(bf16[256,2048]{1,0:T(8,128)(2,1)} %get-tuple-element.22), channel_id=1, source_target_pairs={{0,4},{1,5},{2,6},{3,7},{4,8},{5,9},{6,10},{7,11},{8,12},{9,13},{1... | collective-permute-start | bytes 3145736 | tf_op jit(solution)/shard_map/ppermute | solution.py:209
  47.9 76.0 %all-to-all-start = ((bf16[8,2,64,1024]{3,2,1,0:T(8,128)(2,1)}), bf16[8,2,64,1024]{3,2,1,0:T(8,128)(2,1)S(1)}, u32[]{:S(2)}, u32[]{:S(2)}) async-start(bf16[8,2,64,1024]{3,2,1,0:T(8,128)(2,1)} %get-tuple-element.12), calls=%async_computation | async-start | bytes 4194304 | tf_op jit(solution)/shard_map/all_to_all | solution.py:217
  54.5 40.4 %collective-permute-start.7 = (bf16[256,2048]{1,0:T(8,128)(2,1)}, bf16[256,2048]{1,0:T(8,128)(2,1)}, u32[]{:S(2)}, u32[]{:S(2)}) collective-permute-start(bf16[256,2048]{1,0:T(8,128)(2,1)} %get-tuple-element.23), channel_id=1, source_target_pairs={{0,12},{1,13},{2,14},{3,15},{4,0},{5,1},{6,2},{7,3},{8,4},{9,5},{1... | collective-permute-start | bytes 3145736 | tf_op jit(solution)/shard_map/ppermute | solution.py:210
  61.2 36.0 %copy-start.1 = (bf16[16,8,16,128]{3,1,2,0:T(8,128)(2,1)}, bf16[16,8,16,128]{3,1,2,0:T(8,128)(2,1)S(1)}, u32[]{:S(2)}) copy-start(bf16[16,8,16,128]{3,1,2,0:T(8,128)(2,1)S(1)} %copy.13) | copy-start | bytes 1572868
  61.2 33.2 %collective-permute-start.3 = (bf16[128,2048]{1,0:T(8,128)(2,1)S(1)}, bf16[128,2048]{1,0:T(8,128)(2,1)S(1)}, u32[]{:S(2)}, u32[]{:S(2)}) collective-permute-start(bf16[128,2048]{1,0:T(8,128)(2,1)S(1)} %bitcast.16), channel_id=1, source_target_pairs={{0,2},{1,3},{2,0},{3,1},{4,6},{5,7},{6,4},{7,5},{8,10},{9,11},{10,... | collective-permute-start | bytes 1572872 | tf_op jit(solution)/shard_map/ppermute | solution.py:220
  71.9 44.0 %collective-permute-start.12 = (bf16[256,2048]{1,0:T(8,128)(2,1)}, bf16[256,2048]{1,0:T(8,128)(2,1)}, u32[]{:S(2)}, u32[]{:S(2)}) collective-permute-start(bf16[256,2048]{1,0:T(8,128)(2,1)} %collective-permute-done.5.refs_5_), channel_id=1, source_target_pairs={{0,4},{1,5},{2,6},{3,7},{4,8},{5,9},{6,10},{7,11},{8,12},{9,13},{1... | collective-permute-start | bytes 3145736 | tf_op jit(solution)/shard_map/ppermute | solution.py:211
  71.9 44.0 %collective-permute-start.13 = (bf16[256,2048]{1,0:T(8,128)(2,1)}, bf16[256,2048]{1,0:T(8,128)(2,1)}, u32[]{:S(2)}, u32[]{:S(2)}) collective-permute-start(bf16[256,2048]{1,0:T(8,128)(2,1)} %collective-permute-done.8.refs_8_), channel_id=1, source_target_pairs={{0,12},{1,13},{2,14},{3,15},{4,0},{5,1},{6,2},{7,3},{8,4},{9,5},{1... | collective-permute-start | bytes 3145736 | tf_op jit(solution)/shard_map/ppermute | solution.py:212
  94.4 1.9 %collective-permute-start.2 = (bf16[128,2048]{1,0:T(8,128)(2,1)S(1)}, bf16[128,2048]{1,0:T(8,128)(2,1)S(1)}, u32[]{:S(2)}, u32[]{:S(2)}) collective-permute-start(bf16[128,2048]{1,0:T(8,128)(2,1)S(1)} %bitcast.17), channel_id=1, source_target_pairs={{0,1},{1,0},{2,3},{3,2},{4,5},{5,4},{6,7},{7,6},{8,9},{9,8},{10,11... | collective-permute-start | bytes 1572872 | tf_op jit(solution)/shard_map/ppermute | solution.py:221
  94.4 2.8 %collective-permute-start.4 = (bf16[128,2048]{1,0:T(8,128)(2,1)S(1)}, bf16[128,2048]{1,0:T(8,128)(2,1)}, u32[]{:S(2)}, u32[]{:S(2)}) collective-permute-start(bf16[128,2048]{1,0:T(8,128)(2,1)S(1)} %collective-permute-done.3.refs_2_), channel_id=1, source_target_pairs={{0,1},{1,0},{2,3},{3,2},{4,5},{5,4},{6,7},{7,6},{8,9},{9,8},{10,11... | collective-permute-start | bytes 1572872 | tf_op jit(solution)/shard_map/ppermute | solution.py:222
  106.9 14.4 %collective-permute-start.9 = (bf16[128,1536]{1,0:T(8,128)(2,1)}, bf16[128,1536]{1,0:T(8,128)(2,1)S(1)}, u32[]{:S(2)}, u32[]{:S(2)}) collective-permute-start(bf16[128,1536]{1,0:T(8,128)(2,1)} %get-tuple-element.15), channel_id=1, source_target_pairs={{0,1},{1,0},{2,3},{3,2},{4,5},{5,4},{6,7},{7,6},{8,9},{9,8},{10,11... | collective-permute-start | bytes 1179656 | tf_op jit(solution)/shard_map/ppermute | solution.py:229
  107.1 18.3 %collective-permute-start.10 = (bf16[128,1536]{1,0:T(8,128)(2,1)}, bf16[128,1536]{1,0:T(8,128)(2,1)S(1)}, u32[]{:S(2)}, u32[]{:S(2)}) collective-permute-start(bf16[128,1536]{1,0:T(8,128)(2,1)} %get-tuple-element.16), channel_id=1, source_target_pairs={{0,2},{1,3},{2,0},{3,1},{4,6},{5,7},{6,4},{7,5},{8,10},{9,11},{10,... | collective-permute-start | bytes 1179656 | tf_op jit(solution)/shard_map/ppermute | solution.py:227
  107.1 20.3 %collective-permute-start.11 = (bf16[128,1536]{1,0:T(8,128)(2,1)}, bf16[128,1536]{1,0:T(8,128)(2,1)S(1)}, u32[]{:S(2)}, u32[]{:S(2)}) collective-permute-start(bf16[128,1536]{1,0:T(8,128)(2,1)} %get-tuple-element.17), channel_id=1, source_target_pairs={{0,3},{1,2},{2,1},{3,0},{4,7},{5,6},{6,5},{7,4},{8,11},{9,10},{10,... | collective-permute-start | bytes 1179656 | tf_op jit(solution)/shard_map/ppermute | solution.py:228
  121.0 6.4 %collective-permute-start.14 = (bf16[128,512]{1,0:T(8,128)(2,1)}, bf16[128,512]{1,0:T(8,128)(2,1)S(1)}, u32[]{:S(2)}, u32[]{:S(2)}) collective-permute-start(bf16[128,512]{1,0:T(8,128)(2,1)} %get-tuple-element.19), channel_id=1, source_target_pairs={{0,1},{1,0},{2,3},{3,2},{4,5},{5,4},{6,7},{7,6},{8,9},{9,8},{10,11... | collective-permute-start | bytes 393224 | tf_op jit(solution)/shard_map/ppermute | solution.py:229
  121.1 7.7 %collective-permute-start.15 = (bf16[128,512]{1,0:T(8,128)(2,1)}, bf16[128,512]{1,0:T(8,128)(2,1)S(1)}, u32[]{:S(2)}, u32[]{:S(2)}) collective-permute-start(bf16[128,512]{1,0:T(8,128)(2,1)} %get-tuple-element.20), channel_id=1, source_target_pairs={{0,2},{1,3},{2,0},{3,1},{4,6},{5,7},{6,4},{7,5},{8,10},{9,11},{10,... | collective-permute-start | bytes 393224 | tf_op jit(solution)/shard_map/ppermute | solution.py:227
  121.3 11.0 %collective-permute-start.16 = (bf16[128,512]{1,0:T(8,128)(2,1)}, bf16[128,512]{1,0:T(8,128)(2,1)}, u32[]{:S(2)}, u32[]{:S(2)}) collective-permute-start(bf16[128,512]{1,0:T(8,128)(2,1)} %get-tuple-element.21), channel_id=1, source_target_pairs={{0,3},{1,2},{2,1},{3,0},{4,7},{5,6},{6,5},{7,4},{8,11},{9,10},{10,... | collective-permute-start | bytes 393224 | tf_op jit(solution)/shard_map/ppermute | solution.py:228
  125.4 6.9 %copy-start.5 = (bf16[128,1536]{1,0:T(8,128)(2,1)}, bf16[128,1536]{1,0:T(8,128)(2,1)S(1)}, u32[]{:S(2)}) copy-start(bf16[128,1536]{1,0:T(8,128)(2,1)S(1)} %collective-permute-done.10.refs_2_) | copy-start | bytes 1179652
  127.4 4.9 %copy-start.6 = (bf16[128,1536]{1,0:T(8,128)(2,1)}, bf16[128,1536]{1,0:T(8,128)(2,1)S(1)}, u32[]{:S(2)}) copy-start(bf16[128,1536]{1,0:T(8,128)(2,1)S(1)} %collective-permute-done.11.refs_3_) | copy-start | bytes 1179652
  (6 other events, 16.8 us)

commit v2 on v1

--- a/solution.py
+++ b/solution.py
@@ -23,9 +23,27 @@
     return lax.dot_general(a, b, (((ca,), (cb,)), ((), ())), preferred_element_type=jnp.float32)
 
 
-def attention_kernel(len_ref, odd_ref, q_ref, do_ref, a_ref, b_ref, dq_ref, gkv_ref, k_s, v_s, kt_s, dk_s, dv_s):
+def attention_kernel(len_ref, odd_ref, q_ref, do_ref, a_ref, b_ref, stay_ref, c0_ref, c1_ref, gkv_ref, k_s, v_s, kt_s, dk_s, dv_s):
     step = pl.program_id(1)
-    live = len_ref[pl.program_id(0)]
+    rollout = pl.program_id(0)
+    live = len_ref[rollout]
+    side = odd_ref[1]
+
+    def put(block, head, value):
+        value = value.reshape(BI // BAND, BAND, -1)
+        cols = slice(head * HD, head * HD + value.shape[2])
+        half, first = divmod(block * BI // BAND, N_SEQ // 2)
+        bands = slice(first, first + BI // BAND)
+
+        @pl.when(side == half)
+        def _():
+            stay_ref[bands, 0, :, cols] = value
+
+        for r, ref in enumerate((c0_ref, c1_ref)):
+
+            @pl.when((side != half) & (rollout == r))
+            def _():
+                ref[bands, :, cols] = value
 
     @pl.when(step == 0)
     def _():
@@ -49,7 +67,6 @@
 
     for block in range(ROWS // BI):
         lo, hi = block * BI, (block + 1) * BI
-        bands = slice(lo // BAND, hi // BAND)
 
         @pl.when(live > lo)
         def _():
@@ -77,13 +94,12 @@
                 part = dot(kt_s[:, span], grad_score, 1, 0)
                 dqt = part if dqt is None else dqt + part
             dqt = dqt * SCALE
-            for head in range(HEADS_A_STEP):
-                dq = dqt[:, head * BI : (head + 1) * BI].T.astype(jnp.bfloat16)
-                dq_ref[bands, 0, :, head * HD : (head + 1) * HD] = dq.reshape(BI // BAND, BAND, HD)
+            dq = [dqt[:, head * BI : (head + 1) * BI].T.astype(jnp.bfloat16) for head in range(HEADS_A_STEP)]
+            put(block, 0, jnp.concatenate(dq, axis=1))
 
         @pl.when(live <= lo)
         def _():
-            dq_ref[bands] = jnp.zeros((BI // BAND, 1, BAND, HEADS_A_STEP * HD), jnp.bfloat16)
+            put(block, 0, jnp.zeros((BI, HEADS_A_STEP * HD), jnp.bfloat16))
 
     @pl.when(step == pl.num_programs(1) - 1)
     def _():
@@ -99,7 +115,9 @@
     return pl.pallas_call(
         attention_kernel,
         out_shape=(
-            jax.ShapeDtypeStruct((N_SEQ, rollouts, BAND, GROUP * HD), jnp.bfloat16),
+            jax.ShapeDtypeStruct((N_SEQ // 2, rollouts, BAND, GROUP * HD), jnp.bfloat16),
+            jax.ShapeDtypeStruct((N_SEQ // 2, BAND, GROUP * HD), jnp.bfloat16),
+            jax.ShapeDtypeStruct((N_SEQ // 2, BAND, GROUP * HD), jnp.bfloat16),
             jax.ShapeDtypeStruct((N_SEQ, rollouts, BAND, 2 * HD), jnp.bfloat16),
         ),
         grid_spec=pltpu.PrefetchScalarGridSpec(
@@ -107,7 +125,9 @@
             grid=(rollouts, GROUP // HEADS_A_STEP),
             in_specs=[rows, rows, whole, whole],
             out_specs=[
-                pl.BlockSpec((N_SEQ, 1, BAND, wide), lambda r, h, *_: (0, r, 0, h)),
+                pl.BlockSpec((N_SEQ // 2, 1, BAND, wide), lambda r, h, *_: (0, r, 0, h)),
+                pl.BlockSpec((N_SEQ // 2, BAND, wide), lambda r, h, *_: (0, 0, h)),
+                pl.BlockSpec((N_SEQ // 2, BAND, wide), lambda r, h, *_: (0, 0, h)),
                 pl.BlockSpec((N_SEQ, 1, BAND, 2 * HD), lambda r, h, *_: (0, r, 0, 0)),
             ],
             scratch_shapes=[
@@ -123,13 +143,13 @@
 
 
 def project_kernel(*refs):
-    gs, outs, (g_s, w_s, sems) = refs[:4], refs[-7:-3], refs[-3:]
-    weights = refs[4:-7]
+    gs, outs, (g_s, w_s, sems) = refs[:2], refs[-5:-3], refs[-3:]
+    weights = refs[2:-5]
     rows = gs[0].shape[0]
     starts = [sum(w.shape[0] for w in weights[:i]) for i in range(len(weights) + 1)]
     spans = [slice(a, b) for a, b in zip(starts, starts[1:])]
     loads = [pltpu.make_async_copy(g, g_s.at[i * rows : (i + 1) * rows], sems.at[i]) for i, g in enumerate(gs)]
-    copies = [pltpu.make_async_copy(w, w_s.at[span], sems.at[4 + i]) for i, (w, span) in enumerate(zip(weights, spans))]
+    copies = [pltpu.make_async_copy(w, w_s.at[span], sems.at[2 + i]) for i, (w, span) in enumerate(zip(weights, spans))]
     for copy in loads + copies:
         copy.start()
     for copy in loads:
@@ -147,14 +167,15 @@
     stay = pl.BlockSpec(memory_space=pl.ANY)
     return pl.pallas_call(
         project_kernel,
-        out_shape=(jax.ShapeDtypeStruct((rows, cols), jnp.bfloat16),) * 4,
-        in_specs=[stay] * (4 + len(weights)),
-        out_specs=[pl.BlockSpec(memory_space=pltpu.VMEM)] * 4,
+        out_shape=(jax.ShapeDtypeStruct((rows, cols), jnp.bfloat16),) * 2,
+        in_specs=[stay] * (2 + len(weights)),
+        out_specs=[pl.BlockSpec(memory_space=pltpu.VMEM)] * 2,
         scratch_shapes=[
-            pltpu.VMEM((4 * rows, depth), jnp.bfloat16),
+            pltpu.VMEM((2 * rows, depth), jnp.bfloat16),
             pltpu.VMEM((cols, depth), jnp.bfloat16),
-            pltpu.SemaphoreType.DMA((4 + len(weights),)),
+            pltpu.SemaphoreType.DMA((2 + len(weights),)),
         ],
+        compiler_params=pltpu.CompilerParams(vmem_limit_bytes=20 << 20),
         name="project",
     )(*pieces, *weights)
 
@@ -162,13 +183,12 @@
 def assemble_kernel(at_ref, *refs):
     x, q = at_ref[0], at_ref[1]
     o_ref = refs[-1]
-    for chunk, steps in enumerate(STEPS):
-        for k in range(4):
-            block = refs[4 * chunk + k]
-            shard = block.shape[1] // len(steps)
-            for i, step in enumerate(steps):
-                col = pl.multiple_of(((x + step) % 4 * 4 + (q ^ k)) * shard, shard)
-                o_ref[:, pl.ds(col, shard)] = block[:, i * shard : (i + 1) * shard]
+    for block, (k, pieces) in zip(refs, BLOCKS):
+        start = 0
+        for step, first, width in pieces:
+            col = pl.multiple_of(((x + step) % 4 * 4 + (q ^ k)) * SHARD + first, HALF)
+            o_ref[:, pl.ds(col, width)] = block[:, start : start + width]
+            start += width
 
 
 def assemble(at, blocks):
@@ -180,6 +200,7 @@
         out_shape=jax.ShapeDtypeStruct((rows, cols), jnp.bfloat16),
         in_specs=[pl.BlockSpec(memory_space=pltpu.SMEM)] + [vmem] * len(blocks),
         out_specs=vmem,
+        compiler_params=pltpu.CompilerParams(vmem_limit_bytes=16 << 20),
         name="assemble",
     )(at, *blocks)
 
@@ -189,7 +210,13 @@
 CORE = [(f, f ^ 1) for f in range(16)]
 NEAR = [(f, f ^ 2) for f in range(16)]
 DIAGONAL = [(f, f ^ 3) for f in range(16)]
-STEPS = ((0, 3, 1), (2,))
+SHARD, HALF = 512, 256
+THREE = ((0, 0, SHARD), (3, 0, SHARD), (1, 0, SHARD))
+EARLY = ((0, 0, SHARD), (3, 0, HALF), (1, HALF, HALF))
+LATE = ((3, HALF, HALF), (1, 0, HALF), (2, 0, SHARD))
+BLOCKS = ((0, EARLY), (1, EARLY), (2, THREE), (3, THREE), (2, ((2, 0, SHARD),)), (3, ((2, 0, SHARD),)), (0, LATE), (1, LATE))
+OTHER_HALF = [(s, s ^ 4) for s in range(8)]
+HALVES = [[0, 1, 2, 3], [4, 5, 6, 7]]
 FIRST = [(t, 2 * t) for t in range(4)] + [(4 + t, 2 * t + 1) for t in range(4)]
 SECOND = [(t, 2 * t + 1) for t in range(4)] + [(4 + t, 2 * t) for t in range(4)]
 
@@ -210,25 +237,33 @@
     down0 = lax.ppermute(w0, "fsdp", X_DOWN)
     across0 = lax.ppermute(up0, "fsdp", X_UP)
     across1 = lax.ppermute(down1, "fsdp", X_DOWN)
-    odd = (seq % 2).astype(jnp.int32).reshape(1)
+    odd = jnp.stack([seq % 2, seq // 4]).astype(jnp.int32)
     at = jnp.stack([fsdp // 4, fsdp % 4]).astype(jnp.int32)
-    dq, gkv = attention(lengths, odd, queries, d_out, a, b)
+    stay, c0, c1, gkv = attention(lengths, odd, queries, d_out, a, b)
     gkv = lax.all_to_all(gkv, "seq", split_axis=0, concat_axis=0, tiled=True)
-    dq = lax.all_to_all(dq, "seq", split_axis=0, concat_axis=0, tiled=True)
+    c0 = lax.ppermute(c0, "seq", OTHER_HALF)
+    c1 = lax.ppermute(c1, "seq", OTHER_HALF)
+    stay = lax.all_to_all(stay, "seq", 0, 0, axis_index_groups=HALVES, tiled=True)
+    cross = jnp.stack([c0, c1], axis=1)
+    cross = lax.all_to_all(cross, "seq", 0, 0, axis_index_groups=HALVES, tiled=True)
     rows = rollouts * BAND
     g = gkv.reshape(N_SEQ, rows, 2, HD).transpose(1, 2, 0, 3).reshape(rows, 2 * N_SEQ * HD)
     g_near = lax.ppermute(g, "fsdp", NEAR)
     g_core = lax.ppermute(g, "fsdp", CORE)
     g_far = lax.ppermute(g_near, "fsdp", CORE)
-    pieces = (g, g_core, g_near, g_far)
-    blocks = []
+    own, core = project((g, g_core), (w_kv, up0, down1))
+    core = lax.ppermute(core, "fsdp", CORE)
+    blocks = [own, core]
     for weights in ((w_kv, up0, up1, down0, down1), (across0, across1)):
-        own, core, near, far = project(pieces, weights)
+        near, far = project((g_near, g_far), weights)
         near = lax.ppermute(near, "fsdp", NEAR)
         far = lax.ppermute(far, "fsdp", DIAGONAL)
-        core = lax.ppermute(core, "fsdp", CORE)
-        blocks += [own, core, near, far]
+        blocks += [near, far]
+    own, core = project((g, g_core), (up1, down0, across0, across1))
+    core = lax.ppermute(core, "fsdp", CORE)
+    blocks += [own, core]
     d_hidden = assemble(at, blocks).reshape(rollouts, BAND, -1)
+    dq = jnp.where(seq < 4, jnp.concatenate([stay, cross]), jnp.concatenate([cross, stay]))
     d_queries = dq.transpose(1, 2, 0, 3).reshape(rollouts, BAND, -1)
     return d_queries, d_hidden
 

time: 136 us -> 142 us (1.044)
  waiting for transfers between devices: 57.9 us -> 31.1 us
  starting transfers between devices: 46.1 us -> 72.7 us
  other arithmetic: 1.62 us -> 4.54 us
  local copies, waits for them, and re-layouts: 5.51 us -> 8.05 us
    ppermute x1, waiting for transfers between devices: 19.8 us -> 0.01 us  [body(): up1 = lax.ppermute(w1, 'fsdp', X_UP)]
    ppermute x1, starting transfers between devices: 0.01 us -> 15.7 us  [body(): g_core = lax.ppermute(g, 'fsdp', CORE)]
    ppermute x1, waiting for transfers between devices: 0.01 us -> 14.1 us  [body(): across1 = lax.ppermute(down1, 'fsdp', X_DOWN)]
    ppermute x1, waiting for transfers between devices: 12.3 us -> 0.08 us  [body(): b = lax.ppermute(jnp.where(holds_keys, high, low), 'seq', SECOND)]
    ppermute x1, waiting for transfers between devices: 10.6 us -> 0.01 us  [body(): up0 = lax.ppermute(w0, 'fsdp', X_UP)]
    ppermute x1, waiting for transfers between devices: 0.01 us -> 8.97 us  [body(): down0 = lax.ppermute(w0, 'fsdp', X_DOWN)]
    ppermute x1, starting transfers between devices: 10.3 us -> 2.48 us  [body(): down1 = lax.ppermute(w1, 'fsdp', X_DOWN)]
    ppermute x1, waiting for transfers between devices: 6.78 us -> 0.01 us  [body(): across0 = lax.ppermute(up0, 'fsdp', X_UP)]
  transfers between devices with their start and end apart: 19 -> 22, of which waited for: 9 -> 5; matrix products, arithmetic and copies ran while one was open for 3% -> 7% of each run, Pallas kernels for 11% -> 16%
where the time goes in v2:
time: 142 us
  starting transfers between devices  72.7 us (51%)
  waiting for transfers between devices  31.1 us (22%)
  Pallas kernels  24.6 us (17%)
  local copies, waits for them, and re-layouts  8.05 us (6%)
  other arithmetic  4.54 us (3%)
    pallas_call x4, Pallas kernels, project(): pl.pallas_call(project_kernel, out_shape=(jax.ShapeDtypeStruct((rows, col...  16.4 us
    ppermute x1, starting transfers between devices, body(): g_core = lax.ppermute(g, 'fsdp', CORE)  15.7 us
    ppermute x1, waiting for transfers between devices, body(): across1 = lax.ppermute(down1, 'fsdp', X_DOWN)  14.1 us
    all_to_all x1, starting transfers between devices, body(): gkv = lax.all_to_all(gkv, 'seq', split_axis=0, concat_axis=0, tiled=True)  13.5 us
    ppermute x1, waiting for transfers between devices, body(): down0 = lax.ppermute(w0, 'fsdp', X_DOWN)  8.97 us
    ppermute x1, starting transfers between devices, body(): down0 = lax.ppermute(w0, 'fsdp', X_DOWN)  7.32 us
    pallas_call x1, Pallas kernels, attention(): pl.pallas_call(attention_kernel, out_shape=(jax.ShapeDtypeStruct((N_SEQ /...  5.76 us
    all_to_all x1, waiting for transfers between devices, body(): gkv = lax.all_to_all(gkv, 'seq', split_axis=0, concat_axis=0, tiled=True)  5.64 us
  transfers between devices with their start and end apart: 22, of which 5 were waited for; matrix products, arithmetic and copies ran while one was open for 7% of the time, Pallas kernels for 16%

profile of v2, /device:TPU:1, one launch (start us, length us, event | category | flops | bytes accessed | tf_op | source)
XLA Modules:
  0.0 141.8 jit_solution(18209591362652780825)
XLA Ops:
  1.7 2.5 %collective-permute-start.1 = (bf16[2,512,128]{2,1,0:T(8,128)(2,1)S(1)}, bf16[2,512,128]{2,1,0:T(8,128)(2,1)S(1)}, u32[]{:S(2)}, u32[]{:S(2)}) collective-permute-start(bf16[2,512,128]{2,1,0:T(8,128)(2,1)S(1)} %get-tuple-element.28), channel_id=1, source_target_pairs={{0,16},{16,48},{32,80},{48,112},{64,0},{80,32},{96,64},{112,96},{1... | collective-permute-start | bytes 786440 | tf_op jit(solution)/shard_map/ppermute | solution.py:231
  4.9 3.1 %fusion.1 = (bf16[256,2048]{1,0:T(8,128)(2,1)}, bf16[256,2048]{1,0:T(8,128)(2,1)}) fusion(bf16[512,2048]{1,0:T(8,128)(2,1)} %refs_2_.3), kind=kLoop, calls=%fused_computation.8 | loop fusion | bytes 4194304 | tf_op jit(solution)/shard_map/slice | solution.py:233
  8.1 2.5 %collective-permute-start.6 = (bf16[256,2048]{1,0:T(8,128)(2,1)}, bf16[256,2048]{1,0:T(8,128)(2,1)}, u32[]{:S(2)}, u32[]{:S(2)}) collective-permute-start(bf16[256,2048]{1,0:T(8,128)(2,1)} %get-tuple-element.26), channel_id=1, source_target_pairs={{0,12},{1,13},{2,14},{3,15},{4,0},{5,1},{6,2},{7,3},{8,4},{9,5},{1... | collective-permute-start | bytes 3145736 | tf_op jit(solution)/shard_map/ppermute | solution.py:235
  12.7 5.8 %attention.1 = (bf16[4,2,64,1024]{3,2,1,0:T(8,128)(2,1)}, bf16[4,64,1024]{2,1,0:T(8,128)(2,1)}, bf16[4,64,1024]{2,1,0:T(8,128)(2,1)}, bf16[8,2,64,256]{3,2,1,0:T(8,128)(2,1)}) custom-call(s32[2]{0:T(128)} %len_ref.1, s32[2]{0:T(128)} %pad_add_fusion.odd_ref, bf16[2,512,1024]{2,1,0:T(8,128)(2,1)} %q_ref.1, bf16[2,512,1024]{2,1,0:T(8,128)(2,1)} %do_ref.1, ...), custom_call_target="tpu_custom_call" | custom-call | tf_op jit(solution)/shard_map/attention/pallas_call | solution.py:115
  18.5 13.5 %all-to-all-start.2 = ((bf16[8,2,64,256]{3,2,1,0:T(8,128)(2,1)}), bf16[8,2,64,256]{3,2,1,0:T(8,128)(2,1)S(1)}, u32[]{:S(2)}, u32[]{:S(2)}) async-start(bf16[8,2,64,256]{3,2,1,0:T(8,128)(2,1)} %get-tuple-element.17), calls=%async_computation.2 | async-start | bytes 1048576 | tf_op jit(solution)/shard_map/all_to_all | solution.py:243
  31.9 3.0 %collective-permute-start.2 = (bf16[4,64,1024]{2,1,0:T(8,128)(2,1)}, bf16[4,64,1024]{2,1,0:T(8,128)(2,1)S(1)}, u32[]{:S(2)}, u32[]{:S(2)}) collective-permute-start(bf16[4,64,1024]{2,1,0:T(8,128)(2,1)} %get-tuple-element.15), channel_id=1, source_target_pairs={{0,64},{16,80},{32,96},{48,112},{64,0},{80,16},{96,32},{112,48},{1... | collective-permute-start | bytes 1572872 | tf_op jit(solution)/shard_map/ppermute | solution.py:244
  34.9 5.6 %all-to-all-done.2 = bf16[8,2,64,256]{3,2,1,0:T(8,128)(2,1)S(1)} async-done(((bf16[8,2,64,256]{3,2,1,0:T(8,128)(2,1)}), bf16[8,2,64,256]{3,2,1,0:T(8,128)(2,1)S(1)}, u32[]{:S(2)}, u32[]{:S(2)}) %all-to-all-start.2) | async-done | bytes 524320 | tf_op jit(solution)/shard_map/all_to_all | solution.py:243
  41.5 5.0 %collective-permute-start.8 = (bf16[128,2048]{1,0:T(8,128)(2,1)S(1)}, bf16[128,2048]{1,0:T(8,128)(2,1)S(1)}, u32[]{:S(2)}, u32[]{:S(2)}) collective-permute-start(bf16[128,2048]{1,0:T(8,128)(2,1)S(1)} %bitcast.19), channel_id=1, source_target_pairs={{0,2},{1,3},{2,0},{3,1},{4,6},{5,7},{6,4},{7,5},{8,10},{9,11},{10,... | collective-permute-start | bytes 1572872 | tf_op jit(solution)/shard_map/ppermute | solution.py:251
  46.5 4.2 %all-to-all-start = ((bf16[4,2,64,1024]{3,2,1,0:T(8,128)(2,1)}), bf16[4,2,64,1024]{3,2,1,0:T(8,128)(2,1)}, u32[]{:S(2)}, u32[]{:S(2)}) async-start(bf16[4,2,64,1024]{3,2,1,0:T(8,128)(2,1)} %get-tuple-element.14), calls=%async_computation | async-start | bytes 2097152 | tf_op jit(solution)/shard_map/all_to_all | solution.py:246
  50.7 4.0 %collective-permute-start.10 = (bf16[256,2048]{1,0:T(8,128)(2,1)}, bf16[256,2048]{1,0:T(8,128)(2,1)}, u32[]{:S(2)}, u32[]{:S(2)}) collective-permute-start(bf16[256,2048]{1,0:T(8,128)(2,1)} %get-tuple-element.26), channel_id=1, source_target_pairs={{0,4},{1,5},{2,6},{3,7},{4,8},{5,9},{6,10},{7,11},{8,12},{9,13},{1... | collective-permute-start | bytes 3145736 | tf_op jit(solution)/shard_map/ppermute | solution.py:236
  54.7 15.7 %collective-permute-start.4 = (bf16[128,2048]{1,0:T(8,128)(2,1)S(1)}, bf16[128,2048]{1,0:T(8,128)(2,1)}, u32[]{:S(2)}, u32[]{:S(2)}) collective-permute-start(bf16[128,2048]{1,0:T(8,128)(2,1)S(1)} %bitcast.20), channel_id=1, source_target_pairs={{0,1},{1,0},{2,3},{3,2},{4,5},{5,4},{6,7},{7,6},{8,9},{9,8},{10,11... | collective-permute-start | bytes 1572872 | tf_op jit(solution)/shard_map/ppermute | solution.py:252
  70.5 7.3 %collective-permute-start.11 = (bf16[256,2048]{1,0:T(8,128)(2,1)}, bf16[256,2048]{1,0:T(8,128)(2,1)}, u32[]{:S(2)}, u32[]{:S(2)}) collective-permute-start(bf16[256,2048]{1,0:T(8,128)(2,1)} %get-tuple-element.27), channel_id=1, source_target_pairs={{0,12},{1,13},{2,14},{3,15},{4,0},{5,1},{6,2},{7,3},{8,4},{9,5},{1... | collective-permute-start | bytes 3145736 | tf_op jit(solution)/shard_map/ppermute | solution.py:237
  80.5 4.2 %all-to-all-start.1 = ((bf16[4,2,64,1024]{3,2,1,0:T(8,128)(2,1)}), bf16[4,2,64,1024]{3,2,1,0:T(8,128)(2,1)}, u32[]{:S(2)}, u32[]{:S(2)}) async-start(bf16[4,2,64,1024]{3,2,1,0:T(8,128)(2,1)} %copy.12), calls=%async_computation.1 | async-start | bytes 2097152 | tf_op jit(solution)/shard_map/all_to_all | solution.py:248
  85.8 4.0 %project.4 = (bf16[128,1024]{1,0:T(8,128)(2,1)S(1)}, bf16[128,1024]{1,0:T(8,128)(2,1)}) custom-call(bf16[128,2048]{1,0:T(8,128)(2,1)S(1)} %bitcast.21, bf16[128,2048]{1,0:T(8,128)(2,1)} %collective-permute-done.4.refs_1_, bf16[512,2048]{1,0:T(8,128)(2,1)S(1)} %copy-done, bf16[256,2048]{1,0:T(8,128)(2,1)} %collective-permute-done.5.refs_3_, ...), custom_call_target="tpu_custom_call" | custom-call | tf_op jit(solution)/shard_map/project/pallas_call | solution.py:168
  89.9 1.7 %collective-permute-start.7 = (bf16[128,1024]{1,0:T(8,128)(2,1)}, bf16[128,1024]{1,0:T(8,128)(2,1)}, u32[]{:S(2)}, u32[]{:S(2)}) collective-permute-start(bf16[128,1024]{1,0:T(8,128)(2,1)} %get-tuple-element.19), channel_id=1, source_target_pairs={{0,1},{1,0},{2,3},{3,2},{4,5},{5,4},{6,7},{7,6},{8,9},{9,8},{10,11... | collective-permute-start | bytes 786440 | tf_op jit(solution)/shard_map/ppermute | solution.py:255
  91.6 9.0 %collective-permute-done.11.refs_5_.refs_3_ = bf16[256,2048]{1,0:T(8,128)(2,1)} collective-permute-done((bf16[256,2048]{1,0:T(8,128)(2,1)}, bf16[256,2048]{1,0:T(8,128)(2,1)}, u32[]{:S(2)}, u32[]{:S(2)}) %collective-permute-start.11) | collective-permute-done | bytes 1048608 | tf_op jit(solution)/shard_map/ppermute | solution.py:237
  100.6 5.2 %project.5 = (bf16[128,1536]{1,0:T(8,128)(2,1)}, bf16[128,1536]{1,0:T(8,128)(2,1)}) custom-call(bf16[128,2048]{1,0:T(8,128)(2,1)S(1)} %collective-permute-done.8.refs_0_, bf16[128,2048]{1,0:T(8,128)(2,1)S(1)} %collective-permute-done.9.refs_1_, bf16[512,2048]{1,0:T(8,128)(2,1)S(1)} %copy-done, bf16[256,2048]{1,0:T(8,128)(2,1)} %collective-permute-done.5.refs_3_, ...), custom_call_target="tpu_custom_call" | custom-call | tf_op jit(solution)/shard_map/project/pallas_call | solution.py:168
  105.9 3.0 %collective-permute-start.13 = (bf16[128,1536]{1,0:T(8,128)(2,1)}, bf16[128,1536]{1,0:T(8,128)(2,1)S(1)}, u32[]{:S(2)}, u32[]{:S(2)}) collective-permute-start(bf16[128,1536]{1,0:T(8,128)(2,1)} %get-tuple-element.21), channel_id=1, source_target_pairs={{0,3},{1,2},{2,1},{3,0},{4,7},{5,6},{6,5},{7,4},{8,11},{9,10},{10,... | collective-permute-start | bytes 1179656 | tf_op jit(solution)/shard_map/ppermute | solution.py:260
  108.9 14.1 %collective-permute-done.15.refs_3_.refs_5_ = bf16[256,2048]{1,0:T(8,128)(2,1)} collective-permute-done((bf16[256,2048]{1,0:T(8,128)(2,1)}, bf16[256,2048]{1,0:T(8,128)(2,1)}, u32[]{:S(2)}, u32[]{:S(2)}) %collective-permute-start.15) | collective-permute-done | bytes 1048608 | tf_op jit(solution)/shard_map/ppermute | solution.py:239
  123.1 4.4 %project.7 = (bf16[128,1024]{1,0:T(8,128)(2,1)S(1)}, bf16[128,1024]{1,0:T(8,128)(2,1)S(1)}) custom-call(bf16[128,2048]{1,0:T(8,128)(2,1)S(1)} %bitcast.22, bf16[128,2048]{1,0:T(8,128)(2,1)} %collective-permute-done.4.refs_1_, bf16[256,2048]{1,0:T(8,128)(2,1)} %collective-permute-done.10.refs_4_.refs_2_, ...), custom_call_target="tpu_custom_call" | custom-call | tf_op jit(solution)/shard_map/project/pallas_call | solution.py:168
  128.5 2.8 %project.6 = (bf16[128,512]{1,0:T(8,128)(2,1)S(1)}, bf16[128,512]{1,0:T(8,128)(2,1)S(1)}) custom-call(bf16[128,2048]{1,0:T(8,128)(2,1)S(1)} %collective-permute-done.8.refs_0_, bf16[128,2048]{1,0:T(8,128)(2,1)S(1)} %copy-done.2, bf16[256,2048]{1,0:T(8,128)(2,1)} %collective-permute-done.14.refs_2_.refs_4_, ...), custom_call_target="tpu_custom_call" | custom-call | tf_op jit(solution)/shard_map/project/pallas_call | solution.py:168
  133.0 2.6 %fusion = bf16[8,2,8,8,1024]{4,3,2,1,0:T(8,128)(2,1)S(1)} fusion(bf16[4,2,64,1024]{3,2,1,0:T(8,128)(2,1)} %all-to-all-done.1, bf16[4,2,64,1024]{3,2,1,0:T(8,128)(2,1)} %all-to-all-done, pred[]{:T(512)S(6)} %lt.14), kind=kLoop, calls=%fused_computation.1 | loop fusion | flops 3145728 | bytes 4194305
  137.2 2.2 %collective-permute-done.17.refs_5_ = bf16[128,512]{1,0:T(8,128)(2,1)S(1)} collective-permute-done((bf16[128,512]{1,0:T(8,128)(2,1)S(1)}, bf16[128,512]{1,0:T(8,128)(2,1)S(1)}, u32[]{:S(2)}, u32[]{:S(2)}) %collective-permute-start.17) | collective-permute-done | bytes 131104 | tf_op jit(solution)/shard_map/ppermute | solution.py:260
  139.4 2.5 %assemble.1 = bf16[128,8192]{1,0:T(8,128)(2,1)} custom-call(s32[2]{0:T(128)S(1)} %pad_add_fusion.1.at_ref, bf16[128,1024]{1,0:T(8,128)(2,1)S(1)} %get-tuple-element.18.refs_0_, bf16[128,1024]{1,0:T(8,128)(2,1)} %collective-permute-done.7.refs_1_, bf16[128,1536]{1,0:T(8,128)(2,1)S(1)} %collective-permute-done.12.refs_2_, ...), custom_call_target="tpu_custom_call" | custom-call | tf_op jit(solution)/shard_map/assemble/pallas_call | solution.py:198
  (47 shorter events, 13.0 us)
Async XLA Ops:
  1.7 9.6 %collective-permute-start.1 = (bf16[2,512,128]{2,1,0:T(8,128)(2,1)S(1)}, bf16[2,512,128]{2,1,0:T(8,128)(2,1)S(1)}, u32[]{:S(2)}, u32[]{:S(2)}) collective-permute-start(bf16[2,512,128]{2,1,0:T(8,128)(2,1)S(1)} %get-tuple-element.28), channel_id=1, source_target_pairs={{0,16},{16,48},{32,80},{48,112},{64,0},{80,32},{96,64},{112,96},{1... | collective-permute-start | bytes 786440 | tf_op jit(solution)/shard_map/ppermute | solution.py:231
  4.3 7.0 %collective-permute-start = (bf16[2,512,128]{2,1,0:T(8,128)(2,1)S(1)}, bf16[2,512,128]{2,1,0:T(8,128)(2,1)S(1)}, u32[]{:S(2)}, u32[]{:S(2)}) collective-permute-start(bf16[2,512,128]{2,1,0:T(8,128)(2,1)S(1)} %get-tuple-element.29), channel_id=1, source_target_pairs={{0,0},{16,32},{32,64},{48,96},{64,16},{80,48},{96,80},{112,112},{1... | collective-permute-start | bytes 786440 | tf_op jit(solution)/shard_map/ppermute | solution.py:230
  8.1 62.4 %collective-permute-start.6 = (bf16[256,2048]{1,0:T(8,128)(2,1)}, bf16[256,2048]{1,0:T(8,128)(2,1)}, u32[]{:S(2)}, u32[]{:S(2)}) collective-permute-start(bf16[256,2048]{1,0:T(8,128)(2,1)} %get-tuple-element.26), channel_id=1, source_target_pairs={{0,12},{1,13},{2,14},{3,15},{4,0},{5,1},{6,2},{7,3},{8,4},{9,5},{1... | collective-permute-start | bytes 3145736 | tf_op jit(solution)/shard_map/ppermute | solution.py:235
  10.6 67.2 %collective-permute-start.5 = (bf16[256,2048]{1,0:T(8,128)(2,1)}, bf16[256,2048]{1,0:T(8,128)(2,1)}, u32[]{:S(2)}, u32[]{:S(2)}) collective-permute-start(bf16[256,2048]{1,0:T(8,128)(2,1)} %get-tuple-element.27), channel_id=1, source_target_pairs={{0,4},{1,5},{2,6},{3,7},{4,8},{5,9},{6,10},{7,11},{8,12},{9,13},{1... | collective-permute-start | bytes 3145736 | tf_op jit(solution)/shard_map/ppermute | solution.py:234
  18.5 22.1 %all-to-all-start.2 = ((bf16[8,2,64,256]{3,2,1,0:T(8,128)(2,1)}), bf16[8,2,64,256]{3,2,1,0:T(8,128)(2,1)S(1)}, u32[]{:S(2)}, u32[]{:S(2)}) async-start(bf16[8,2,64,256]{3,2,1,0:T(8,128)(2,1)} %get-tuple-element.17), calls=%async_computation.2 | async-start | bytes 1048576 | tf_op jit(solution)/shard_map/all_to_all | solution.py:243
  31.9 18.8 %collective-permute-start.2 = (bf16[4,64,1024]{2,1,0:T(8,128)(2,1)}, bf16[4,64,1024]{2,1,0:T(8,128)(2,1)S(1)}, u32[]{:S(2)}, u32[]{:S(2)}) collective-permute-start(bf16[4,64,1024]{2,1,0:T(8,128)(2,1)} %get-tuple-element.15), channel_id=1, source_target_pairs={{0,64},{16,80},{32,96},{48,112},{64,0},{80,16},{96,32},{112,48},{1... | collective-permute-start | bytes 1572872 | tf_op jit(solution)/shard_map/ppermute | solution.py:244
  34.9 19.8 %collective-permute-start.3 = (bf16[4,64,1024]{2,1,0:T(8,128)(2,1)}, bf16[4,64,1024]{2,1,0:T(8,128)(2,1)S(1)}, u32[]{:S(2)}, u32[]{:S(2)}) collective-permute-start(bf16[4,64,1024]{2,1,0:T(8,128)(2,1)} %get-tuple-element.16), channel_id=1, source_target_pairs={{0,64},{16,80},{32,96},{48,112},{64,0},{80,16},{96,32},{112,48},{1... | collective-permute-start | bytes 1572872 | tf_op jit(solution)/shard_map/ppermute | solution.py:245
  41.5 36.4 %collective-permute-start.8 = (bf16[128,2048]{1,0:T(8,128)(2,1)S(1)}, bf16[128,2048]{1,0:T(8,128)(2,1)S(1)}, u32[]{:S(2)}, u32[]{:S(2)}) collective-permute-start(bf16[128,2048]{1,0:T(8,128)(2,1)S(1)} %bitcast.19), channel_id=1, source_target_pairs={{0,2},{1,3},{2,0},{3,1},{4,6},{5,7},{6,4},{7,5},{8,10},{9,11},{10,... | collective-permute-start | bytes 1572872 | tf_op jit(solution)/shard_map/ppermute | solution.py:251
  46.5 34.0 %all-to-all-start = ((bf16[4,2,64,1024]{3,2,1,0:T(8,128)(2,1)}), bf16[4,2,64,1024]{3,2,1,0:T(8,128)(2,1)}, u32[]{:S(2)}, u32[]{:S(2)}) async-start(bf16[4,2,64,1024]{3,2,1,0:T(8,128)(2,1)} %get-tuple-element.14), calls=%async_computation | async-start | bytes 2097152 | tf_op jit(solution)/shard_map/all_to_all | solution.py:246
  50.7 39.2 %collective-permute-start.10 = (bf16[256,2048]{1,0:T(8,128)(2,1)}, bf16[256,2048]{1,0:T(8,128)(2,1)}, u32[]{:S(2)}, u32[]{:S(2)}) collective-permute-start(bf16[256,2048]{1,0:T(8,128)(2,1)} %get-tuple-element.26), channel_id=1, source_target_pairs={{0,4},{1,5},{2,6},{3,7},{4,8},{5,9},{6,10},{7,11},{8,12},{9,13},{1... | collective-permute-start | bytes 3145736 | tf_op jit(solution)/shard_map/ppermute | solution.py:236
  54.7 30.0 %collective-permute-start.4 = (bf16[128,2048]{1,0:T(8,128)(2,1)S(1)}, bf16[128,2048]{1,0:T(8,128)(2,1)}, u32[]{:S(2)}, u32[]{:S(2)}) collective-permute-start(bf16[128,2048]{1,0:T(8,128)(2,1)S(1)} %bitcast.20), channel_id=1, source_target_pairs={{0,1},{1,0},{2,3},{3,2},{4,5},{5,4},{6,7},{7,6},{8,9},{9,8},{10,11... | collective-permute-start | bytes 1572872 | tf_op jit(solution)/shard_map/ppermute | solution.py:252
  70.5 30.1 %collective-permute-start.11 = (bf16[256,2048]{1,0:T(8,128)(2,1)}, bf16[256,2048]{1,0:T(8,128)(2,1)}, u32[]{:S(2)}, u32[]{:S(2)}) collective-permute-start(bf16[256,2048]{1,0:T(8,128)(2,1)} %get-tuple-element.27), channel_id=1, source_target_pairs={{0,12},{1,13},{2,14},{3,15},{4,0},{5,1},{6,2},{7,3},{8,4},{9,5},{1... | collective-permute-start | bytes 3145736 | tf_op jit(solution)/shard_map/ppermute | solution.py:237
  77.8 45.3 %collective-permute-start.15 = (bf16[256,2048]{1,0:T(8,128)(2,1)}, bf16[256,2048]{1,0:T(8,128)(2,1)}, u32[]{:S(2)}, u32[]{:S(2)}) collective-permute-start(bf16[256,2048]{1,0:T(8,128)(2,1)} %collective-permute-done.6.refs_4_.refs_6_), channel_id=1, source_target_pairs={{0,12},{1,13},{2,14},{3,15},{4,0},{5,1},{6,2},{7,3},{8,4},{9,5},{1... | collective-permute-start | bytes 3145736 | tf_op jit(solution)/shard_map/ppermute | solution.py:239
  77.9 45.2 %collective-permute-start.14 = (bf16[256,2048]{1,0:T(8,128)(2,1)}, bf16[256,2048]{1,0:T(8,128)(2,1)}, u32[]{:S(2)}, u32[]{:S(2)}) collective-permute-start(bf16[256,2048]{1,0:T(8,128)(2,1)} %collective-permute-done.5.refs_3_), channel_id=1, source_target_pairs={{0,4},{1,5},{2,6},{3,7},{4,8},{5,9},{6,10},{7,11},{8,12},{9,13},{1... | collective-permute-start | bytes 3145736 | tf_op jit(solution)/shard_map/ppermute | solution.py:238
  79.4 6.5 %copy-start = (bf16[512,2048]{1,0:T(8,128)(2,1)S(1)}, bf16[512,2048]{1,0:T(8,128)(2,1)}, u32[]{:S(2)}) copy-start(bf16[512,2048]{1,0:T(8,128)(2,1)} %refs_2_.3) | copy-start | bytes 6291460
  80.5 52.5 %all-to-all-start.1 = ((bf16[4,2,64,1024]{3,2,1,0:T(8,128)(2,1)}), bf16[4,2,64,1024]{3,2,1,0:T(8,128)(2,1)}, u32[]{:S(2)}, u32[]{:S(2)}) async-start(bf16[4,2,64,1024]{3,2,1,0:T(8,128)(2,1)} %copy.12), calls=%async_computation.1 | async-start | bytes 2097152 | tf_op jit(solution)/shard_map/all_to_all | solution.py:248
  84.7 15.9 %collective-permute-start.9 = (bf16[128,2048]{1,0:T(8,128)(2,1)S(1)}, bf16[128,2048]{1,0:T(8,128)(2,1)S(1)}, u32[]{:S(2)}, u32[]{:S(2)}) collective-permute-start(bf16[128,2048]{1,0:T(8,128)(2,1)S(1)} %collective-permute-done.8.refs_0_), channel_id=1, source_target_pairs={{0,1},{1,0},{2,3},{3,2},{4,5},{5,4},{6,7},{7,6},{8,9},{9,8},{10,11... | collective-permute-start | bytes 1572872 | tf_op jit(solution)/shard_map/ppermute | solution.py:253
  89.9 41.5 %collective-permute-start.7 = (bf16[128,1024]{1,0:T(8,128)(2,1)}, bf16[128,1024]{1,0:T(8,128)(2,1)}, u32[]{:S(2)}, u32[]{:S(2)}) collective-permute-start(bf16[128,1024]{1,0:T(8,128)(2,1)} %get-tuple-element.19), channel_id=1, source_target_pairs={{0,1},{1,0},{2,3},{3,2},{4,5},{5,4},{6,7},{7,6},{8,9},{9,8},{10,11... | collective-permute-start | bytes 786440 | tf_op jit(solution)/shard_map/ppermute | solution.py:255
  105.9 31.3 %collective-permute-start.12 = (bf16[128,1536]{1,0:T(8,128)(2,1)}, bf16[128,1536]{1,0:T(8,128)(2,1)S(1)}, u32[]{:S(2)}, u32[]{:S(2)}) collective-permute-start(bf16[128,1536]{1,0:T(8,128)(2,1)} %get-tuple-element.20), channel_id=1, source_target_pairs={{0,2},{1,3},{2,0},{3,1},{4,6},{5,7},{6,4},{7,5},{8,10},{9,11},{10,... | collective-permute-start | bytes 1179656 | tf_op jit(solution)/shard_map/ppermute | solution.py:259
  105.9 31.2 %collective-permute-start.13 = (bf16[128,1536]{1,0:T(8,128)(2,1)}, bf16[128,1536]{1,0:T(8,128)(2,1)S(1)}, u32[]{:S(2)}, u32[]{:S(2)}) collective-permute-start(bf16[128,1536]{1,0:T(8,128)(2,1)} %get-tuple-element.21), channel_id=1, source_target_pairs={{0,3},{1,2},{2,1},{3,0},{4,7},{5,6},{6,5},{7,4},{8,11},{9,10},{10,... | collective-permute-start | bytes 1179656 | tf_op jit(solution)/shard_map/ppermute | solution.py:260
  108.9 19.6 %copy-start.2 = (bf16[128,2048]{1,0:T(8,128)(2,1)S(1)}, bf16[128,2048]{1,0:T(8,128)(2,1)}, u32[]{:S(2)}) copy-start(bf16[128,2048]{1,0:T(8,128)(2,1)} %copy-done.1) | copy-start | bytes 1572868
  127.4 11.9 %collective-permute-start.18 = (bf16[128,1024]{1,0:T(8,128)(2,1)S(1)}, bf16[128,1024]{1,0:T(8,128)(2,1)S(1)}, u32[]{:S(2)}, u32[]{:S(2)}) collective-permute-start(bf16[128,1024]{1,0:T(8,128)(2,1)S(1)} %get-tuple-element.25), channel_id=1, source_target_pairs={{0,1},{1,0},{2,3},{3,2},{4,5},{5,4},{6,7},{7,6},{8,9},{9,8},{10,11... | collective-permute-start | bytes 786440 | tf_op jit(solution)/shard_map/ppermute | solution.py:263
  131.3 5.9 %collective-permute-start.16 = (bf16[128,512]{1,0:T(8,128)(2,1)S(1)}, bf16[128,512]{1,0:T(8,128)(2,1)S(1)}, u32[]{:S(2)}, u32[]{:S(2)}) collective-permute-start(bf16[128,512]{1,0:T(8,128)(2,1)S(1)} %get-tuple-element.22), channel_id=1, source_target_pairs={{0,2},{1,3},{2,0},{3,1},{4,6},{5,7},{6,4},{7,5},{8,10},{9,11},{10,... | collective-permute-start | bytes 393224 | tf_op jit(solution)/shard_map/ppermute | solution.py:259
  131.4 8.0 %collective-permute-start.17 = (bf16[128,512]{1,0:T(8,128)(2,1)S(1)}, bf16[128,512]{1,0:T(8,128)(2,1)S(1)}, u32[]{:S(2)}, u32[]{:S(2)}) collective-permute-start(bf16[128,512]{1,0:T(8,128)(2,1)S(1)} %get-tuple-element.23), channel_id=1, source_target_pairs={{0,3},{1,2},{2,1},{3,0},{4,7},{5,6},{6,5},{7,4},{8,11},{9,10},{10,... | collective-permute-start | bytes 393224 | tf_op jit(solution)/shard_map/ppermute | solution.py:260
  (3 other events, 6.7 us)
